TPU v7x, 256 devices: a whole 4x4x8 slice. The times are simulated.
256 devices in a mesh: tok: 64 (over x, z, core), ch: 4 (over y).
Axes of the slice: x: 4, y: 4, z: 8, core: 2. Of those that a mesh axis runs over, the one named last changes fastest.
Arguments:
- inputs: float32 [65536, 1024], P('tok', 'ch'), may hold values from -6 to 6
- factor_one: float32 [512, 512], replicated, may hold values from -0.25 to 0.25
- twiddle: float32 [128, 512], P('tok'), may hold values from -4 to 4
- factor_two: float32 [128, 128], replicated, may hold values from -0.5 to 0.5
- w_up: bfloat16 [4, 256, 1024], P('ch', 'tok'), may hold values from -0.375 to 0.375
- w_down: bfloat16 [4, 1024, 256], P('ch', 'tok'), may hold values from -0.1875 to 0.1875
- out_cotangent: float32 [65536, 1024], P('tok', 'ch'), may hold values from -6 to 6
Outputs:
- outputs: float32 [65536, 1024], P('tok', 'ch')
- grad_inputs: float32 [65536, 1024], P('tok', 'ch')
- grad_factor_one: float32 [512, 512], replicated
- grad_factor_two: float32 [128, 128], replicated
- grad_up: float32 [4, 256, 1024], P('ch', 'tok')
- grad_down: float32 [4, 1024, 256], P('ch', 'tok')
All inputs are finite; a program needn't handle non-finite values.
Results may differ from a plain program's by a relative error of at most 0.0057.
Values may be sent and summed in bfloat16 or wider, within the bound.
A program may use at most 64 MiB of HBM per device.

v0:
```python
import math

import jax
import jax.numpy as jnp
from jax import lax
from jax.sharding import PartitionSpec as P

inv_root_two = 1.0 / math.sqrt(2.0)
inv_root_tau = 1.0 / math.sqrt(2.0 * math.pi)


def gelu_parts(value):
    cdf = 0.5 * (1.0 + jax.scipy.special.erf(value * inv_root_two))
    return (value * cdf, cdf + value * jnp.exp(-0.5 * value * value) * inv_root_tau)


def to_columns(block):
    count = lax.axis_size("tok")
    rows, width, chans = block.shape
    return lax.all_to_all(
        block.reshape(rows, count, width // count, chans),
        "tok",
        split_axis=1,
        concat_axis=0,
        tiled=True,
    ).reshape(count * rows, width // count, chans)


def to_rows(block):
    return lax.all_to_all(block, "tok", split_axis=0, concat_axis=1, tiled=True)


def local(inputs, factor_one, twiddle, factor_two, w_up, w_down, out_cotangent):
    high = lax.Precision.HIGHEST
    rows = twiddle.shape[0]
    width = twiddle.shape[1]
    chans = inputs.shape[1]
    panels = (
        lax.all_gather(w_up, "tok", axis=1, tiled=True),
        lax.all_gather(w_down, "tok", axis=1, tiled=True),
    )
    up_w = panels[0][0]
    down_w = panels[1][0]
    grid = inputs.reshape(rows, width, chans)
    first = jnp.einsum("kj,ijc->ikc", factor_one, grid, precision=high)
    mid = first * twiddle[:, :, None]
    mid_cols = to_columns(mid)
    mixed_cols = jnp.einsum("mi,ikc->mkc", factor_two, mid_cols, precision=high)
    mixed = to_rows(mixed_cols).reshape(rows * width, chans)
    gate = jax.nn.sigmoid(inputs)
    branch = inputs + gate * mixed
    normed = branch.astype(jnp.bfloat16)
    up = jnp.dot(normed, up_w, preferred_element_type=jnp.float32)
    active, slope = gelu_parts(up)
    hidden = active.astype(jnp.bfloat16)
    outputs = branch + jnp.dot(hidden, down_w, preferred_element_type=jnp.float32)
    cot = out_cotangent.astype(jnp.bfloat16)
    d_hidden = jnp.dot(cot, down_w.T, preferred_element_type=jnp.float32)
    d_up = (d_hidden * slope).astype(jnp.bfloat16)
    d_branch = out_cotangent + jnp.dot(d_up, up_w.T, preferred_element_type=jnp.float32)
    grad_down_part = jnp.dot(hidden.T, cot, preferred_element_type=jnp.float32)
    grad_up_part = jnp.dot(normed.T, d_up, preferred_element_type=jnp.float32)
    grad_up, grad_down = (
        lax.psum_scatter(grad_up_part[None], "tok", scatter_dimension=1, tiled=True),
        lax.psum_scatter(grad_down_part[None], "tok", scatter_dimension=1, tiled=True),
    )
    d_mixed = d_branch * gate
    direct = d_branch * (1.0 + gate * (1.0 - gate) * mixed)
    cot_cols = to_columns(d_mixed.reshape(rows, width, chans))
    d_mid_cols = jnp.einsum("mi,mkc->ikc", factor_two, cot_cols, precision=high)
    two_part = jnp.einsum("mkc,ikc->mi", cot_cols, mid_cols, precision=high)
    d_first = to_rows(d_mid_cols) * twiddle[:, :, None]
    one_part = jnp.einsum("ikc,ijc->kj", d_first, grid, precision=high)
    d_grid = jnp.einsum("kj,ikc->ijc", factor_one, d_first, precision=high)
    grad_inputs = direct + d_grid.reshape(rows * width, chans)
    grad_one, grad_two = lax.psum((one_part, two_part), ("tok", "ch"))
    return (outputs, grad_inputs, grad_one, grad_two, grad_up, grad_down)


def solution(mesh):
    in_specs = (
        P("tok", "ch"),
        P(),
        P("tok", None),
        P(),
        P("ch", "tok", None),
        P("ch", "tok", None),
        P("tok", "ch"),
    )
    out_specs = (
        P("tok", "ch"),
        P("tok", "ch"),
        P(),
        P(),
        P("ch", "tok", None),
        P("ch", "tok", None),
    )
    return jax.shard_map(local, mesh=mesh, in_specs=in_specs, out_specs=out_specs, check_vma=False)
```

profile of v0, /device:TPU:1, one launch (start us, length us, event | category | flops | bytes accessed | tf_op | source)
XLA Modules:
  0.0 718.6 jit_solution(10194359381156684317)
XLA Ops:
  8.0 1.2 copy-done
  9.2 4.7 fusion.6
  14.5 41.5 %all_to_all.63 = f32[2,64,8,256]{3,2,0,1:T(8,128)S(1)} all-to-all(f32[2,64,8,256]{3,2,0,1:T(8,128)S(1)} %copy.66), channel_id=1, replica_groups=mesh['tok'=64,'ch'=4] {'tok'}, dimensions={1} | all-to-all | bytes 2097152 | tf_op jit(solution)/shard_map/all_to_all | solution.py:20
  55.9 1.0 copy-done.4
  56.9 1.9 convolution_bitcast_fusion.5
  58.9 1.4 copy.68
  60.2 6.2 all-to-all-start.1
  66.5 73.7 %all_gather.6 = bf16[1,256,1024]{2,0,1:T(2,128)(2,1)} all-gather(bf16[1,4,1024]{2,0,1:T(2,128)(2,1)S(1)} %copy.70), channel_id=1, replica_groups=mesh['tok'=64,'ch'=4] {'tok'}, dimensions={1}, use_global_device_ids=true | all-gather | bytes 532480 | tf_op jit(solution)/shard_map/all_gather | solution.py:39
  140.2 54.0 %all_gather.7 = bf16[1,1024,256]{2,1,0:T(8,128)(2,1)} all-gather(bf16[1,16,256]{2,1,0:T(8,128)(2,1)S(1)} %copy-done.11), channel_id=1, replica_groups=mesh['tok'=64,'ch'=4] {'tok'}, dimensions={1}, use_global_device_ids=true | all-gather | bytes 532480 | tf_op jit(solution)/shard_map/all_gather | solution.py:40
  194.3 1.0 copy-done.2
  195.8 2.4 multiply_convert_fusion
  198.2 2.2 fusion.5
  200.4 1.8 fusion.33
  202.3 35.6 %all_to_all.64 = f32[2,64,8,256]{3,2,0,1:T(8,128)S(1)} all-to-all(f32[2,64,8,256]{3,2,0,1:T(8,128)S(1)} %copy.71), channel_id=1, replica_groups=mesh['tok'=64,'ch'=4] {'tok'}, dimensions={1} | all-to-all | bytes 2097152 | tf_op jit(solution)/shard_map/all_to_all | solution.py:20
  237.9 1.1 copy-done.5
  238.9 2.9 convolution_bitcast_fusion.4
  241.8 2.7 copy.73
  244.5 6.4 all-to-all-start.3
  250.9 3.3 convolution_bitcast_fusion.1
  254.3 3.6 convolution_bitcast_fusion
  259.4 3.4 convolution_add_fusion.1
  262.8 180.2 %all-reduce.5.cloned.1.call-done = f32[1,256,1024]{2,1,0:T(8,128)} async-done(((f32[1,256,1024]{2,1,0:T(8,128)}), f32[1,256,1024]{2,1,0:T(8,128)}) %all-reduce.5.cloned.1.call-update) | async-done | bytes 1048592
  443.0 1.4 constant_dynamic-slice_fusion
  444.4 3.6 convolution_bitcast_fusion.6
  448.0 4.2 convolution_bitcast_fusion.2
  452.3 4.4 convolution_bitcast_fusion.3
  456.6 2.6 copy.76
  459.2 2.9 fusion.10
  462.1 119.3 %reduce-scatter.3.cloned.1.call-done = f32[1,16,256]{2,1,0:T(8,128)} async-done(((f32[1,1024,256]{2,1,0:T(8,128)}), f32[1,16,256]{2,1,0:T(8,128)}) %reduce-scatter.3.cloned.1.call-update) | async-done | bytes 16400 | tf_op jit(solution)/shard_map/reduce_scatter | solution.py:65
  581.4 126.0 %all-reduce.7.cloned.1.call-done = (f32[512,512]{1,0:T(8,128)}, f32[128,128]{1,0:T(8,128)}) async-done(((f32[512,512]{1,0:T(8,128)}, f32[128,128]{1,0:T(8,128)}), (f32[512,512]{1,0:T(8,128)}, f32[128,128]{1,0:T(8,128)})) %all-reduce.7.cloned.1.call-update) | async-done | bytes 1114128 | tf_op jit(solution)/shard_map/psum | solution.py:76
  707.4 2.3 copy.110
  709.7 1.5 copy.111
  (41 shorter events, 2.2 us)
Async XLA Ops:
  8.0 1.2 copy-start
  9.2 47.7 %copy-start.9 = (f32[128,128]{1,0:T(8,128)S(1)}, f32[128,128]{1,0:T(8,128)}, u32[]{:S(2)}) copy-start(f32[128,128]{1,0:T(8,128)} %param.10) | copy-start | bytes 196612
  14.5 52.0 %copy-start.12 = (bf16[1,4,1024]{2,1,0:T(4,128)(2,1)S(1)}, bf16[1,4,1024]{2,1,0:T(4,128)(2,1)}, u32[]{:S(2)}) copy-start(bf16[1,4,1024]{2,1,0:T(4,128)(2,1)} %param.11) | copy-start | bytes 24580
  55.9 1.0 copy-start.4
  55.9 84.2 %copy-start.11 = (bf16[1,16,256]{2,1,0:T(8,128)(2,1)S(1)}, bf16[1,16,256]{2,1,0:T(8,128)(2,1)}, u32[]{:S(2)}) copy-start(bf16[1,16,256]{2,1,0:T(8,128)(2,1)} %param.12) | copy-start | bytes 24580
  58.8 136.4 %copy-start.1 = (f32[1024,256]{1,0:T(8,128)S(1)}, f32[1024,256]{1,0:T(8,128)}, u32[]{:S(2)}) copy-start(f32[1024,256]{1,0:T(8,128)} %param.7) | copy-start | bytes 3145732
  60.2 134.0 %all-to-all-start.1 = ((f32[128,8,256]{2,1,0:T(8,128)}), f32[128,8,256]{2,1,0:T(8,128)S(1)}, u32[]{:S(2)}, u32[]{:S(2)}) async-start(f32[128,8,256]{2,1,0:T(8,128)} %copy.68), calls=%async_computation.1 | async-start | bytes 2097152 | tf_op jit(solution)/shard_map/all_to_all | solution.py:30
  194.2 1.6 copy-start.6
  194.3 1.0 copy-start.2
  195.8 2.4 copy-start.8
  195.8 2.4 copy-start.13
  200.4 1.8 copy-start.7
  237.9 1.1 copy-start.5
  244.5 203.5 %all-to-all-start.3 = ((f32[128,8,256]{2,1,0:T(8,128)}), f32[128,8,256]{2,1,0:T(8,128)}, u32[]{:S(2)}, u32[]{:S(2)}) async-start(f32[128,8,256]{2,1,0:T(8,128)} %copy.73), calls=%async_computation.3 | async-start | bytes 2097152 | tf_op jit(solution)/shard_map/all_to_all | solution.py:30
  250.9 192.1 %all-reduce.5.cloned.1.call-start = ((), (), s32[]{:S(2)}) async-start(), calls=%async_computation.6 | async-start | bytes 2097152
  254.2 4.0 copy-start.14
  254.3 327.2 %reduce-scatter.3.cloned.1.call-start = ((), (), s32[]{:S(2)}) async-start(), calls=%async_computation.5 | async-start | bytes 1064960 | tf_op jit(solution)/shard_map/reduce_scatter | solution.py:65
  257.9 449.5 %all-reduce.7.cloned.1.call-start = ((), (), s32[]{:S(2)}) async-start(), calls=%async_computation.7 | async-start | bytes 2228224 | tf_op jit(solution)/shard_map/psum | solution.py:76
  259.4 188.6 %copy-start.10 = (f32[2,512]{1,0:T(2,128)S(1)}, f32[2,512]{1,0:T(2,128)}, u32[]{:S(2)}) copy-start(f32[2,512]{1,0:T(2,128)} %param.9) | copy-start | bytes 12292
  448.0 11.2 %copy-start.3 = (f32[2,64,8,256]{3,2,1,0:T(8,128)S(1)}, f32[2,64,8,256]{3,2,1,0:T(8,128)}, u32[]{:S(2)}) copy-start(f32[2,64,8,256]{3,2,1,0:T(8,128)} %copy-done.2) | copy-start | bytes 3145732
Sparse Core Ops, SparseCore 0:
  256.1 186.8 all-reduce.4
  447.6 133.7 reduce-scatter.2
Sparse Core Ops, SparseCore 1:
  452.3 255.0 all-reduce.6
where the time goes:
time: 720 us; the launch traced here: 719 us
  waiting for transfers between devices  426 us (59%)
  blocking collectives  205 us (28%)
  matrix products  38.3 us (5%)
  local copies, waits for them, and re-layouts  17.5 us (2%)
  between operations  16.3 us (2%)
  starting transfers between devices  12.9 us (2%)
    unnamed x4, waiting for transfers between devices  180 us
    psum x1, waiting for transfers between devices, local(): grad_one, grad_two = lax.psum((one_part, two_part), ('tok', 'ch'))  126 us
    reduce_scatter x1, waiting for transfers between devices, local(): lax.psum_scatter(grad_down_part[None], 'tok', scatter_dimension=1, tiled=...  119 us
    all_to_all x2, blocking collectives, to_columns(): lax.all_to_all(block.reshape(rows, count, width // count, chans), 'tok',...  77.1 us
    all_gather x1, blocking collectives, local(): lax.all_gather(w_up, 'tok', axis=1, tiled=True)  73.7 us
    all_gather x1, blocking collectives, local(): lax.all_gather(w_down, 'tok', axis=1, tiled=True)  54 us
  transfers between devices with their start and end apart: 5, of which 3 were waited for; matrix products, arithmetic and copies ran while one was open for 4% of the time, Pallas kernels for 0%

commit v1 on v0

v1 whole, which is shorter than its diff:
```python
import functools
import math

import jax
import jax.numpy as jnp
from jax import lax
from jax.experimental import pallas as pl
from jax.experimental.pallas import tpu as pltpu
from jax.sharding import PartitionSpec as P

inv_root_two = 1.0 / math.sqrt(2.0)
inv_root_tau = 1.0 / math.sqrt(2.0 * math.pi)
f32 = jnp.float32
bf16 = jnp.bfloat16

A1, A2, A3, A4, WZ, WX, WC, GC, GX, GZ, TC, TZ, TX, TY, TZ2, TC2, PC, PY, PQ, PQ2, PY2, PC2 = range(22)


def gelu_parts(value):
    cdf = 0.5 * (1.0 + lax.erf(value * inv_root_two))
    return (value * cdf, cdf + value * jnp.exp(-0.5 * value * value) * inv_root_tau)


def mm(a, b):
    return jnp.dot(a, b, preferred_element_type=f32)


def mm_nt(a, b):
    return lax.dot_general(a, b, (((1,), (1,)), ((), ())), preferred_element_type=f32)


def mm_tn(a, b):
    return lax.dot_general(a, b, (((0,), (0,)), ((), ())), preferred_element_type=f32)


def split(a):
    high = a.astype(bf16)
    return high, (a - high.astype(f32)).astype(bf16)


def kernel(X, Z, Y, x_ref, f1_ref, tw_ref, f2_ref, wu_ref, wd_ref, oc_ref,
           out_ref, gx_ref, g1_ref, g2_ref, gu_ref, gd_ref,
           sa, ra, kh, kl, kth, ktl, wbuf, wup, wdn, stage, rows4, dhid, hid, dup, nrm, cot,
           gbuf, rgc, sgx, rgx, sgz, rgz, tpart, rtc, stz, rtz, rtx, rty, rt2,
           ppart, rpc, spy, rpy, spq, rpq, fin, fy, wpack, ssem, rsem):
    NQ = X * Z
    nt = 2 * NQ
    C = x_ref.shape[3]
    M = 8 * nt
    N = 16 * nt
    R = 2 * nt
    LY = M // Y
    W = min(C, 128)
    t = lax.axis_index("tok")
    y = lax.axis_index("ch")
    core = lax.rem(t, 2)
    q = lax.div(t, 2)
    z = lax.rem(q, Z)
    xx = lax.div(q, Z)
    sib = t + 1 - 2 * core
    other = 1 - core

    def tok_of(x_at, z_at):
        return (x_at * Z + z_at) * 2 + core

    def push(which, src, dst, tok, ch):
        pltpu.make_async_remote_copy(
            src_ref=src, dst_ref=dst, send_sem=ssem.at[which], recv_sem=rsem.at[which],
            device_id=(tok, ch), device_id_type=pl.DeviceIdType.MESH,
        ).start()

    def arrive(which, view):
        pltpu.make_async_copy(view, view, rsem.at[which]).wait()

    def sent(which, view):
        pltpu.make_async_copy(view, view, ssem.at[which]).wait()

    def each(count, body):
        def step(d, carry):
            body(d)
            return carry
        lax.fori_loop(1, count, step, 0)

    barrier = pltpu.get_barrier_semaphore()

    def greet_tok(d):
        pl.semaphore_signal(barrier, inc=1, device_id=(lax.rem(t + d, nt), y), device_id_type=pl.DeviceIdType.MESH)

    def greet_ch(d):
        pl.semaphore_signal(barrier, inc=1, device_id=(t, lax.rem(y + d, Y)), device_id_type=pl.DeviceIdType.MESH)

    each(nt, greet_tok)
    each(Y, greet_ch)

    f1h, f1l = split(f1_ref[...])
    eye = lax.broadcasted_iota(jnp.int32, (M, M), 0) == lax.broadcasted_iota(jnp.int32, (M, M), 1)

    def tw_col(i):
        return jnp.sum(jnp.where(eye, tw_ref[i : i + 1, :], 0.0), axis=1, keepdims=True)

    def pair(a, b):
        n = a.shape[0]
        return jnp.concatenate([a[:, None], b[:, None]], axis=1).reshape(n, 16, C)

    mids = []
    for i in range(2):
        xh, xl = split(x_ref[i].reshape(M, C))
        first = mm(f1h, xh) + mm(f1h, xl) + mm(f1l, xh)
        mids.append((first * tw_col(i)).reshape(nt, 8, C))
    sa[0] = pair(mids[0], mids[1]).astype(bf16)
    ra[0, t] = sa[0, t]

    wpack[...] = jnp.concatenate(
        [wd_ref[...].astype(f32)] + [wu_ref[:, fq * C : (fq + 1) * C].astype(f32) for fq in range(4)], axis=0)
    wbuf[core, xx, z] = wpack[...].astype(bf16)

    pl.semaphore_wait(barrier, nt - 1 + Y - 1)

    def a2a(phase):
        def one(d):
            peer = lax.rem(t + d, nt)
            push(phase, sa.at[phase, peer], ra.at[phase, t], peer, y)
        each(nt, one)

    def a2a_arrive(phase):
        arrive(phase, ra.at[phase, pl.ds(0, nt - 1)])

    a2a(A1)
    each(Z, lambda d: push(WZ, wbuf.at[core, xx, z], wbuf.at[core, xx, z], tok_of(xx, lax.rem(z + d, Z)), y))

    f2h, f2l = split(f2_ref[...])
    f2t = f2_ref[...].T
    f2th, f2tl = split(f2t)
    band = min(N // 2, 128)
    spread = (lax.broadcasted_iota(jnp.int32, (N, R), 0) >> 3) == lax.broadcasted_iota(jnp.int32, (N, R), 1)
    spread = jnp.where(spread, 1.0, 0.0).astype(bf16)

    def build(src, dst):
        def step(b, carry):
            r0 = pl.multiple_of(b * band, band)
            rows = (lax.broadcasted_iota(jnp.int32, (band, R), 0) + r0) >> 3
            pick = jnp.where(rows == lax.broadcasted_iota(jnp.int32, (band, R), 1), 1.0, 0.0).astype(bf16)
            part = mm_nt(mm(pick, src).astype(bf16), spread)
            same = ((lax.broadcasted_iota(jnp.int32, (band, N), 0) & 7)
                    == (lax.broadcasted_iota(jnp.int32, (band, N), 1) & 7))
            dst[pl.ds(r0, band), :] = jnp.where(same, part, 0.0).astype(bf16)
            return carry
        lax.fori_loop(0, N // band, step, 0)

    build(f2h, kh)
    build(f2l, kl)

    arrive(WZ, wbuf.at[core, xx, pl.ds(0, Z - 1)])
    each(X, lambda d: push(WX, wbuf.at[core, xx], wbuf.at[core, xx], tok_of(lax.rem(xx + d, X), z), y))

    a2a_arrive(A1)
    mid = ra[0].reshape(N, C)
    sa[1] = (mm(kh[...], mid) + mm(kl[...], mid)).astype(bf16).reshape(nt, 16, C)
    ra[1, t] = sa[1, t]
    a2a(A2)

    arrive(WX, wbuf.at[core, pl.ds(0, X - 1)])
    push(WC, wbuf.at[core], wbuf.at[core], sib, y)
    build(f2th, kth)
    build(f2tl, ktl)
    arrive(WC, wbuf.at[other])

    for c in range(2):
        wdn[:, c] = wbuf[c, :, :, 0:16].reshape(NQ, 16, C)
    up_rows = [wbuf[c, :, :, 16:32].astype(f32).reshape(NQ, 1, 16, C) for c in range(2)]
    up_rows = jnp.concatenate(up_rows, axis=1).reshape(N, C)
    for h in range(C // W):
        rows4[h] = up_rows[:, h * W : (h + 1) * W]
    for fq in range(4):
        for h in range(C // W):
            for r in range(4):
                stage[pl.ds(r, nt, stride=4), :] = rows4[h, pl.ds(4 * fq + r, nt, stride=16), :]
            wup[:, fq * C + h * W : fq * C + (h + 1) * W] = stage[...].astype(bf16)

    nb = max(1, nt // 4)
    tiles = nt // nb

    def tokens(ref, s0):
        return pair(ref[0, pl.ds(s0, nb)], ref[1, pl.ds(s0, nb)]).reshape(nb * 16, C)

    def put(ref, s0, value):
        value = value.reshape(nb, 2, 8, C)
        ref[0, pl.ds(s0, nb)] = value[:, 0]
        ref[1, pl.ds(s0, nb)] = value[:, 1]

    down = wdn[...].reshape(N, C)

    def pre(j, carry):
        s0 = pl.multiple_of(j * nb, nb)
        r0 = pl.multiple_of(j * nb * 16, nb * 16)
        c16 = tokens(oc_ref, s0).astype(bf16)
        cot[pl.ds(r0, nb * 16), :] = c16
        dhid[pl.ds(r0, nb * 16), :] = mm_nt(c16, wdn[...].reshape(N, C))
        return carry

    lax.fori_loop(0, tiles, pre, 0)

    a2a_arrive(A2)

    def mlp(j, carry):
        tile = lax.rem(lax.div(t, nb) + j, tiles)
        s0 = pl.multiple_of(tile * nb, nb)
        r0 = pl.multiple_of(tile * nb * 16, nb * 16)
        rows = pl.ds(r0, nb * 16)
        mixed = ra[1, pl.ds(s0, nb)].reshape(nb * 16, C).astype(f32)
        inp = tokens(x_ref, s0)
        gate = jax.nn.sigmoid(inp)
        branch = inp + gate * mixed
        normed = branch.astype(bf16)
        nrm[rows, :] = normed
        up = mm(normed, wup[...])
        active, slope = gelu_parts(up)
        hidden = active.astype(bf16)
        hid[rows, :] = hidden
        put(out_ref, s0, branch + mm(hidden, wdn[...].reshape(N, C)))
        d_up = (dhid[rows, :] * slope).astype(bf16)
        dup[rows, :] = d_up
        d_branch = tokens(oc_ref, s0) + mm_nt(d_up, wup[...])
        sa[2, pl.ds(s0, nb)] = (d_branch * gate).astype(bf16).reshape(nb, 16, C)
        put(gx_ref, s0, d_branch * (1.0 + gate * (1.0 - gate) * mixed))

        def one(b, inner):
            peer = s0 + lax.rem(t + b, nb)

            @pl.when(peer != t)
            def _():
                push(A3, sa.at[2, peer], ra.at[2, t], peer, y)

            return inner

        lax.fori_loop(0, nb, one, 0)
        return carry

    lax.fori_loop(0, tiles, mlp, 0)
    ra[2, t] = sa[2, t]

    gd_part = mm_tn(hid[...], cot[...]).reshape(NQ, 2, 16, C)
    for c in range(2):
        gbuf[c, :, 0:16] = gd_part[:, c]
    for fq in range(4):
        gu_part = mm_tn(nrm[...], dup[:, fq * C : (fq + 1) * C])
        for h in range(C // W):
            stage[...] = gu_part[:, h * W : (h + 1) * W]
            for r in range(4):
                rows4[h, pl.ds(4 * fq + r, nt, stride=16), :] = stage[pl.ds(r, nt, stride=4), :]
    for c in range(2):
        for h in range(C // W):
            gbuf[c, :, 16:32, h * W : (h + 1) * W] = rows4[h].reshape(NQ, 2, 16, W)[:, c]
    push(GC, gbuf.at[other], rgc, sib, y)

    a2a_arrive(A3)
    grad = ra[2].reshape(N, C)
    sa[3] = (mm(kth[...], grad) + mm(ktl[...], grad)).astype(bf16).reshape(nt, 16, C)
    ra[3, t] = sa[3, t]
    a2a(A4)

    arrive(GC, rgc)
    sgx[...] = (gbuf[core] + rgc[...]).astype(bf16).reshape(X, Z, 32, C)

    def send_gx(d):
        peer = lax.rem(xx + d, X)
        push(GX, sgx.at[peer], rgx.at[xx], tok_of(peer, z), y)

    each(X, send_gx)

    def two(b, carry):
        r0 = pl.multiple_of(b * band, band)
        prod = mm_nt(ra[2, pl.ds(b * (band // 16), band // 16)].reshape(band, C), ra[0].reshape(N, C))
        same = ((lax.broadcasted_iota(jnp.int32, (band, N), 0) & 7)
                == (lax.broadcasted_iota(jnp.int32, (band, N), 1) & 7))
        ph, pw = split(jnp.where(same, prod, 0.0))
        tpart[b] = (mm(ph, spread) + mm(pw, spread)).reshape(band // 8, 8, R).sum(axis=1)
        return carry

    lax.fori_loop(0, N // band, two, 0)
    half = tpart.shape[0] // 2
    push(TC, tpart.at[pl.ds(other * half, half)], rtc, sib, y)

    arrive(GX, rgx.at[pl.ds(0, X - 1)])
    rgx[xx] = jnp.zeros((Z, 32, C), bf16)
    zrows = pl.ds(xx * Z, Z)
    own_gz = gbuf[core, zrows] + rgc[zrows]
    for s in range(X):
        own_gz = own_gz + rgx[s].astype(f32)
    gbuf[core, zrows] = own_gz
    sgz[...] = own_gz.astype(bf16)

    def send_gz(d):
        peer = lax.rem(z + d, Z)
        push(GZ, sgz.at[peer], rgz.at[z], tok_of(xx, peer), y)

    each(Z, send_gz)

    arrive(TC, rtc)
    stz[...] = (tpart[pl.ds(core * half, half)] + rtc[...]).reshape(Z, nt // Z, R)

    def send_tz(d):
        peer = lax.rem(z + d, Z)
        push(TZ, stz.at[peer], rtz.at[z], tok_of(xx, peer), y)

    each(Z, send_tz)

    arrive(GZ, rgz.at[pl.ds(0, Z - 1)])
    rgz[z] = jnp.zeros((32, C), bf16)
    wpack[...] = gbuf[core, xx * Z + z] + rgz[...].astype(f32).sum(axis=0)
    gd_ref[...] = wpack[0:16, :]
    for fq in range(4):
        gu_ref[:, fq * C : (fq + 1) * C] = wpack[16 + 4 * fq : 20 + 4 * fq, :]

    arrive(TZ, rtz.at[pl.ds(0, Z - 1)])
    rtz[z] = stz[z]
    rtx[xx] = rtz[...].sum(axis=0)
    each(X, lambda d: push(TX, rtx.at[xx], rtx.at[xx], tok_of(lax.rem(xx + d, X), z), y))
    arrive(TX, rtx.at[pl.ds(0, X - 1)])
    rty[y] = rtx[...].sum(axis=0)
    each(Y, lambda d: push(TY, rty.at[y], rty.at[y], t, lax.rem(y + d, Y)))
    arrive(TY, rty.at[pl.ds(0, Y - 1)])
    rt2[core, z] = rty[...].sum(axis=0)
    each(Z, lambda d: push(TZ2, rt2.at[core, z], rt2.at[core, z], tok_of(xx, lax.rem(z + d, Z)), y))

    a2a_arrive(A4)
    d_mid = ra[3].astype(f32).reshape(nt, 2, 8, C)
    d_first = [(d_mid[:, i].reshape(M, C) * tw_col(i)).astype(bf16) for i in range(2)]
    one = mm_nt(d_first[0], x_ref[0].reshape(M, C).astype(bf16)) + mm_nt(d_first[1], x_ref[1].reshape(M, C).astype(bf16))
    one = one.reshape(NQ, 2, 8, M)
    for c in range(2):
        for v in range(Y):
            ppart[c, v] = one[:, c, :, v * LY : (v + 1) * LY]
    push(PC, ppart.at[other], rpc, sib, y)

    arrive(TZ2, rt2.at[core, pl.ds(0, Z - 1)])
    push(TC2, rt2.at[core], rt2.at[core], sib, y)

    f1t = f1_ref[...].T.astype(bf16)
    for i in range(2):
        gx_ref[i] = gx_ref[i] + mm(f1t, d_first[i]).reshape(nt, 8, C)

    arrive(PC, rpc)
    spy[...] = (ppart[core] + rpc[...]).astype(bf16).reshape(Y, NQ * 8, LY)

    def send_py(d):
        peer = lax.rem(y + d, Y)
        push(PY, spy.at[peer], rpy.at[y], t, peer)

    each(Y, send_py)
    arrive(TC2, rt2.at[other])
    g2_ref[...] = rt2[...].reshape(R, R)
    arrive(PY, rpy.at[pl.ds(0, Y - 1)])
    rpy[y] = jnp.zeros((NQ * 8, LY), bf16)
    total = (ppart[core, y] + rpc[y]).reshape(NQ * 8, LY)
    for s in range(Y):
        total = total + rpy[s].astype(f32)
    spq[...] = total.reshape(NQ, 8, LY)

    def send_pq(d):
        peer = lax.rem(q + d, NQ)
        push(PQ, spq.at[peer], rpq.at[q], 2 * peer + core, y)

    each(NQ, send_pq)
    arrive(PQ, rpq.at[pl.ds(0, NQ - 1)])
    rpq[q] = spq[q]
    fin[q] = rpq[...].sum(axis=0).astype(bf16).astype(f32)
    each(NQ, lambda d: push(PQ2, fin.at[q], fin.at[q], 2 * lax.rem(q + d, NQ) + core, y))
    arrive(PQ2, fin.at[pl.ds(0, NQ - 1)])
    fy[core, y] = fin[...].reshape(NQ * 8, LY).astype(bf16)
    each(Y, lambda d: push(PY2, fy.at[core, y], fy.at[core, y], t, lax.rem(y + d, Y)))
    arrive(PY2, fy.at[core, pl.ds(0, Y - 1)])
    push(PC2, fy.at[core], fy.at[core], sib, y)
    arrive(PC2, fy.at[other])
    for c in range(2):
        for v in range(Y):
            g1_ref[:, c, :, v * LY : (v + 1) * LY] = fy[c, v].astype(f32).reshape(NQ, 8, LY)

    for phase in (A1, A2, A3, A4):
        sent(phase, sa.at[phase, pl.ds(0, nt - 1)])
    sent(WZ, wbuf.at[0, 0, pl.ds(0, Z - 1)])
    sent(WX, wbuf.at[0, pl.ds(0, X - 1)])
    sent(WC, wbuf.at[0])
    sent(GC, rgc)
    sent(GX, sgx.at[pl.ds(0, X - 1)])
    sent(GZ, sgz.at[pl.ds(0, Z - 1)])
    sent(TC, rtc)
    sent(TZ, stz.at[pl.ds(0, Z - 1)])
    sent(TX, rtx.at[pl.ds(0, X - 1)])
    sent(TY, rty.at[pl.ds(0, Y - 1)])
    sent(TZ2, rt2.at[0, pl.ds(0, Z - 1)])
    sent(TC2, rt2.at[0])
    sent(PC, rpc)
    sent(PY, spy.at[pl.ds(0, Y - 1)])
    sent(PQ, spq.at[pl.ds(0, NQ - 1)])
    sent(PQ2, fin.at[pl.ds(0, NQ - 1)])
    sent(PY2, fy.at[0, pl.ds(0, Y - 1)])
    sent(PC2, fy.at[0])


def local(X, Z, Y, inputs, factor_one, twiddle, factor_two, w_up, w_down, out_cotangent):
    NQ = X * Z
    nt = 2 * NQ
    C = inputs.shape[1]
    M = 8 * nt
    N = 16 * nt
    R = 2 * nt
    LY = M // Y
    W = min(C, 128)
    band = min(N // 2, 128)
    V = pltpu.VMEM
    scratch = [
        V((4, nt, 16, C), bf16), V((4, nt, 16, C), bf16),
        V((N, N), bf16), V((N, N), bf16), V((N, N), bf16), V((N, N), bf16),
        V((2, X, Z, 32, C), bf16), V((C, 4 * C), bf16), V((NQ, 2, 16, C), bf16),
        V((C, W), f32), V((C // W, N, W), f32),
        V((N, 4 * C), f32), V((N, 4 * C), bf16), V((N, 4 * C), bf16), V((N, C), bf16), V((N, C), bf16),
        V((2, NQ, 32, C), f32), V((NQ, 32, C), f32),
        V((X, Z, 32, C), bf16), V((X, Z, 32, C), bf16), V((Z, 32, C), bf16), V((Z, 32, C), bf16),
        V((N // band, band // 8, R), f32), V((N // band // 2, band // 8, R), f32),
        V((Z, nt // Z, R), f32), V((Z, nt // Z, R), f32), V((X, nt // Z, R), f32), V((Y, nt // Z, R), f32),
        V((2, Z, nt // Z, R), f32),
        V((2, Y, NQ, 8, LY), f32), V((Y, NQ, 8, LY), f32),
        V((Y, NQ * 8, LY), bf16), V((Y, NQ * 8, LY), bf16),
        V((NQ, 8, LY), f32), V((NQ, 8, LY), f32), V((NQ, 8, LY), f32), V((2, Y, NQ * 8, LY), bf16),
        V((32, C), f32),
        pltpu.SemaphoreType.DMA((22,)), pltpu.SemaphoreType.DMA((22,)),
    ]
    shapes = [
        ((2, nt, 8, C), f32), ((2, nt, 8, C), f32), ((NQ, 2, 8, M), f32), ((R, R), f32),
        ((4, 4 * C), f32), ((16, C), f32),
    ]
    vm = pl.BlockSpec(memory_space=pltpu.VMEM)
    out, gx, g1, g2, gu, gd = pl.pallas_call(
        functools.partial(kernel, X, Z, Y),
        out_shape=[jax.ShapeDtypeStruct(*s) for s in shapes],
        in_specs=[vm] * 7,
        out_specs=[vm] * 6,
        scratch_shapes=scratch,
        compiler_params=pltpu.CompilerParams(
            collective_id=0, has_side_effects=True, vmem_limit_bytes=60 * 1024 * 1024),
        name="monarch",
    )(
        inputs.reshape(2, nt, 8, C), factor_one, twiddle, factor_two,
        w_up[0], w_down[0], out_cotangent.reshape(2, nt, 8, C),
    )
    return (out.reshape(2 * M, C), gx.reshape(2 * M, C), g1.reshape(M, M), g2, gu[None], gd[None])


def solution(mesh):
    nt = mesh.shape["tok"]
    Y = mesh.shape["ch"]
    X = 4 if nt == 64 else 2
    in_specs = (
        P("tok", "ch"),
        P(),
        P("tok", None),
        P(),
        P("ch", "tok", None),
        P("ch", "tok", None),
        P("tok", "ch"),
    )
    out_specs = (
        P("tok", "ch"),
        P("tok", "ch"),
        P(),
        P(),
        P("ch", "tok", None),
        P("ch", "tok", None),
    )
    return jax.shard_map(
        functools.partial(local, X, nt // 2 // X, Y), mesh=mesh, in_specs=in_specs, out_specs=out_specs, check_vma=False)
```

time: 720 us -> 134 us (0.19)
  waiting for transfers between devices: 426 us -> 0 us
  blocking collectives: 205 us -> 0 us
  Pallas kernels: 0 us -> 126 us
  matrix products: 38.3 us -> 0 us
  between operations: 16.3 us -> 0.66 us
  starting transfers between devices: 12.9 us -> 0 us
  local copies, waits for them, and re-layouts: 17.5 us -> 6.98 us
    unnamed x4 -> x0, waiting for transfers between devices: 180 us -> none
    all_gather x2 -> x0, blocking collectives: 128 us -> none  [the longest x1 73.7 us: local(): lax.all_gather(w_up, 'tok', axis=1, tiled=True)]
    pallas_call x0 -> x1, Pallas kernels: none -> 126 us  [local(): pl.pallas_call(functools.partial(kernel, X, Z, Y), out_shape=[jax.ShapeDt...]
    psum x1 -> x0, waiting for transfers between devices: 126 us -> none  [local(): grad_one, grad_two = lax.psum((one_part, two_part), ('tok', 'ch'))]
    reduce_scatter x1 -> x0, waiting for transfers between devices: 119 us -> none  [local(): lax.psum_scatter(grad_down_part[None], 'tok', scatter_dimension=1, tiled=...]
    all_to_all x2 -> x0, blocking collectives: 77.1 us -> none  [to_columns(): lax.all_to_all(block.reshape(rows, count, width // count, chans), 'tok',...]
    dot_general x12 -> x0, matrix products: 38.3 us -> none  [the longest x1 4.73 us: local(): first = jnp.einsum('kj,ijc->ikc', factor_one, grid, precision=high)]
    all_to_all x2 -> x0, starting transfers between devices: 12.6 us -> none  [to_rows(): return lax.all_to_all(block, 'tok', split_axis=0, concat_axis=1, tiled=True)]
  transfers between devices with their start and end apart: 5 -> 0, of which waited for: 3 -> 0; matrix products, arithmetic and copies ran while one was open for 4% -> 0% of each run, Pallas kernels for 0% -> 0%
where the time goes in v1:
time: 134 us
  Pallas kernels  126 us (94%)
  local copies, waits for them, and re-layouts  6.98 us (5%)
    pallas_call x1, Pallas kernels, local(): pl.pallas_call(functools.partial(kernel, X, Z, Y), out_shape=[jax.ShapeDt...  126 us
    unnamed x16, local copies, waits for them, and re-layouts  6.98 us

profile of v1, /device:TPU:1, one launch (start us, length us, event | category | flops | bytes accessed | tf_op | source)
XLA Modules:
  0.0 134.0 jit_solution(17178047455081771554)
XLA Ops:
  0.6 126.3 %monarch.1 = (f32[2,64,8,256]{3,2,1,0:T(8,128)}, f32[2,64,8,256]{3,2,1,0:T(8,128)}, f32[32,2,8,512]{3,2,1,0:T(8,128)}, f32[128,128]{1,0:T(8,128)}, f32[4,1024]{1,0:T(4,128)}, /*index=5*/f32[16,256]{1,0:T(8,128)}) custom-call(f32[2,64,8,256]{3,2,1,0:T(8,128)} %bitcast.9, f32[512,512]{1,0:T(8,128)} %f1_ref.1, f32[2,512]{1,0:T(2,128)} %tw_ref.1, ...), custom_call_target="tpu_custom_call" | custom-call | tf_op jit(solution)/shard_map/monarch/pallas_call | solution.py:434
  127.0 0.0 copy-start.1
  127.0 2.4 %copy.19 = f32[1024,256]{1,0:T(8,128)} copy(f32[1024,256]{1,0:T(8,128)} %bitcast.13) | data formatting | bytes 2097152
  129.3 0.0 copy-done.1
  129.3 0.0 copy-start
  129.3 1.0 copy.20
  130.3 0.6 copy-done
  130.9 0.0 copy-start.2
  130.9 1.0 copy.21
  131.9 0.0 copy-done.2
  131.9 0.0 copy-start.4
  131.9 0.6 copy.22
  132.6 0.1 copy-done.4
  132.6 0.0 copy-start.3
  132.6 0.6 copy.23
  133.2 0.1 copy-done.3
  133.4 0.6 copy.24
Async XLA Ops:
  127.0 2.4 %copy-start.1 = (f32[2,64,8,256]{3,2,1,0:T(8,128)S(1)}, f32[2,64,8,256]{3,2,1,0:T(8,128)}, u32[]{:S(2)}) copy-start(f32[2,64,8,256]{3,2,1,0:T(8,128)} %get-tuple-element.13) | copy-start | bytes 3145732
  129.3 1.6 %copy-start = (f32[32,2,8,512]{3,2,1,0:T(8,128)S(1)}, f32[32,2,8,512]{3,2,1,0:T(8,128)}, u32[]{:S(2)}) copy-start(f32[32,2,8,512]{3,2,1,0:T(8,128)} %get-tuple-element.14) | copy-start | bytes 3145732
  130.9 1.0 copy-start.2
  131.9 0.7 copy-start.4
  132.6 0.7 copy-start.3

commit v2 on v1

v2 whole, which is shorter than its diff:
```python
import functools
import math

import jax
import jax.numpy as jnp
from jax import lax
from jax.experimental import pallas as pl
from jax.experimental.pallas import tpu as pltpu
from jax.sharding import PartitionSpec as P

inv_root_two = 1.0 / math.sqrt(2.0)
inv_root_tau = 1.0 / math.sqrt(2.0 * math.pi)
f32 = jnp.float32
bf16 = jnp.bfloat16

(A1, A2, A2B, A3, A4, A4B, WZ, WX, WC, GC, GX, GZ, TC, TZ, TX, TY, TZ2, TC2, PC, PY, PQ, PQ2, PY2, PC2) = range(24)
NEX = 24
LX, LF1, LOC, LTW, LF2, LWU, LWD = range(7)


def gelu_parts(value):
    cdf = 0.5 * (1.0 + lax.erf(value * inv_root_two))
    return (value * cdf, cdf + value * jnp.exp(-0.5 * value * value) * inv_root_tau)


def mm(a, b):
    return jnp.dot(a, b, preferred_element_type=f32)


def mm_nt(a, b):
    return lax.dot_general(a, b, (((1,), (1,)), ((), ())), preferred_element_type=f32)


def mm_tn(a, b):
    return lax.dot_general(a, b, (((0,), (0,)), ((), ())), preferred_element_type=f32)


def split(a):
    high = a.astype(bf16)
    return high, (a - high.astype(f32)).astype(bf16)


def kernel(X, Z, Y, x_in, f1_in, tw_in, f2_in, wu_in, wd_in, oc_in,
           out_ref, gx_ref, fy, g2_ref, gu_ref, gd_ref,
           xv, f1v, ocv, tw_ref, f2v, wu_ref, wd_ref,
           sa, ra, kh, kth, ktl, f1t, xb, twc, wbuf, wup, wdn, stage, rows4, dhid, hid, dup, nrm, cot, df,
           gbuf, rgc, sgx, rgx, sgz, rgz, tsum, tpart, rtc, stz, rtz, rtx, rty, rt2,
           ppart, rpc, spy, rpy, spq, rpq, fin, wpack, ssem, rsem, lsem):
    NQ = X * Z
    nt = 2 * NQ
    C = xv.shape[4]
    M = 8 * nt
    H = 8 * NQ
    N = 16 * nt
    R = 2 * nt
    LY = M // Y
    W = min(C, 128)
    lgq = NQ.bit_length() - 1
    t = lax.axis_index("tok")
    y = lax.axis_index("ch")
    core = lax.rem(t, 2)
    q = lax.div(t, 2)
    z = lax.rem(q, Z)
    xx = lax.div(q, Z)
    sib = t + 1 - 2 * core
    other = 1 - core
    me = core * NQ + q

    def tok_of(x_at, z_at):
        return (x_at * Z + z_at) * 2 + core

    def push(which, src, dst, tok, ch):
        pltpu.make_async_remote_copy(
            src_ref=src, dst_ref=dst, send_sem=ssem.at[which], recv_sem=rsem.at[which],
            device_id=(tok, ch), device_id_type=pl.DeviceIdType.MESH,
        ).start()

    def arrive(which, view):
        pltpu.make_async_copy(view, view, rsem.at[which]).wait()

    def sent(which, view):
        pltpu.make_async_copy(view, view, ssem.at[which]).wait()

    def each(count, body, start=1):
        def step(d, carry):
            body(d)
            return carry
        lax.fori_loop(start, count, step, 0)

    barrier = pltpu.get_barrier_semaphore()

    def greet_tok(d):
        pl.semaphore_signal(barrier, inc=1, device_id=(lax.rem(t + d, nt), y), device_id_type=pl.DeviceIdType.MESH)

    def greet_ch(d):
        pl.semaphore_signal(barrier, inc=1, device_id=(t, lax.rem(y + d, Y)), device_id_type=pl.DeviceIdType.MESH)

    each(nt, greet_tok)
    each(Y, greet_ch)
    loads = {}
    for which, src, dst in ((LF1, f1_in, f1v), (LX, x_in, xv), (LTW, tw_in, tw_ref), (LWU, wu_in, wu_ref),
                            (LWD, wd_in, wd_ref), (LF2, f2_in, f2v), (LOC, oc_in, ocv)):
        loads[which] = pltpu.make_async_copy(src, dst, lsem.at[which])
        loads[which].start()

    loads[LF1].wait()
    f1h, f1l = split(f1v[...])
    loads[LTW].wait()
    eye = lax.broadcasted_iota(jnp.int32, (M, M), 0) == lax.broadcasted_iota(jnp.int32, (M, M), 1)
    for i in range(2):
        col = jnp.sum(jnp.where(eye, tw_ref[i : i + 1, :], 0.0), axis=1, keepdims=True)
        twc[i] = col.reshape(NQ, 2, 8, 1)

    def pair(a, b):
        n = a.shape[0]
        return jnp.concatenate([a[:, None], b[:, None]], axis=1).reshape(n, 16, C)

    loads[LX].wait()
    mids = []
    for i in range(2):
        xh, xl = split(xv[i].reshape(M, C))
        xb[i] = xh
        first = mm(f1h, xh) + mm(f1h, xl) + mm(f1l, xh)
        mids.append(first.reshape(NQ, 2, 8, C) * twc[i])
    for c in range(2):
        sa[0, c * NQ : (c + 1) * NQ] = pair(mids[0][:, c], mids[1][:, c]).astype(bf16)
    ra[0, me] = sa[0, me]

    loads[LWU].wait()
    loads[LWD].wait()
    wpack[...] = jnp.concatenate(
        [wd_ref[...].astype(f32)] + [wu_ref[:, fq * C : (fq + 1) * C].astype(f32) for fq in range(4)], axis=0)
    wbuf[core, xx, z] = wpack[...].astype(bf16)

    pl.semaphore_wait(barrier, nt - 1 + Y - 1)

    def a2a(phase, which):
        for c in range(2):
            def one(d):
                peer = lax.rem(q + d, NQ)

                @pl.when((peer != q) | (core != c))
                def _():
                    push(which, sa.at[phase, c * NQ + peer], ra.at[phase, me], 2 * peer + c, y)

            each(NQ, one, 0)

    def from_core(which, phase, c):
        @pl.when(core == c)
        def _():
            arrive(which, ra.at[phase, pl.ds(0, NQ - 1)])

        @pl.when(core != c)
        def _():
            arrive(which, ra.at[phase, pl.ds(0, NQ)])

    def from_all(which, phase):
        arrive(which, ra.at[phase, pl.ds(0, nt - 1)])

    a2a(0, A1)
    each(Z, lambda d: push(WZ, wbuf.at[core, xx, z], wbuf.at[core, xx, z], tok_of(xx, lax.rem(z + d, Z)), y))

    loads[LF2].wait()
    f2h = f2v[...].astype(bf16)
    f2th, f2tl = split(f2v[...].T)
    band = min(N // 2, 128)

    def row_of(n):
        return 4 * ((n >> 4) & (NQ - 1)) + 2 * (n >> (4 + lgq)) + ((n >> 3) & 1)

    spread = row_of(lax.broadcasted_iota(jnp.int32, (N, R), 0)) == lax.broadcasted_iota(jnp.int32, (N, R), 1)
    spread = jnp.where(spread, 1.0, 0.0).astype(bf16)
    same = ((lax.broadcasted_iota(jnp.int32, (band, N), 0) & 7) == (lax.broadcasted_iota(jnp.int32, (band, N), 1) & 7))

    def picked(r0):
        rows = row_of(lax.broadcasted_iota(jnp.int32, (band, R), 0) + r0)
        return jnp.where(rows == lax.broadcasted_iota(jnp.int32, (band, R), 1), 1.0, 0.0).astype(bf16)

    def build(src, dst):
        def step(b, carry):
            r0 = pl.multiple_of(b * band, band)
            part = mm_nt(mm(picked(r0), src).astype(bf16), spread)
            dst[pl.ds(r0, band), :] = jnp.where(same, part, 0.0).astype(bf16)
            return carry
        lax.fori_loop(0, N // band, step, 0)

    build(f2h, kh)

    arrive(WZ, wbuf.at[core, xx, pl.ds(0, Z - 1)])
    each(X, lambda d: push(WX, wbuf.at[core, xx], wbuf.at[core, xx], tok_of(lax.rem(xx + d, X), z), y))

    from_all(A1, 0)
    sa[1] = mm(kh[...], ra[0].reshape(N, C)).astype(bf16).reshape(nt, 16, C)
    ra[1, me] = sa[1, me]
    a2a(1, A2 + core)

    arrive(WX, wbuf.at[core, pl.ds(0, X - 1)])
    push(WC, wbuf.at[core], wbuf.at[core], sib, y)
    build(f2th, kth)
    build(f2tl, ktl)
    for c in range(2):
        f1t[c] = f1v[...].reshape(NQ, 2, 8, M)[:, c].reshape(H, M).T.astype(bf16)
    arrive(WC, wbuf.at[other])

    for c in range(2):
        wdn[:, c] = wbuf[c, :, :, 0:16].reshape(NQ, 16, C)
    up_rows = [wbuf[c, :, :, 16:32].astype(f32).reshape(NQ, 1, 16, C) for c in range(2)]
    up_rows = jnp.concatenate(up_rows, axis=1).reshape(N, C)
    for h in range(C // W):
        rows4[h] = up_rows[:, h * W : (h + 1) * W]
    for fq in range(4):
        for h in range(C // W):
            for r in range(4):
                stage[pl.ds(r, nt, stride=4), :] = rows4[h, pl.ds(4 * fq + r, nt, stride=16), :]
            wup[:, fq * C + h * W : fq * C + (h + 1) * W] = stage[...].astype(bf16)

    nb = max(1, NQ // 2)
    tiles = NQ // nb
    TB = nb * 16

    def tokens(ref, c, q0):
        return pair(ref[0, pl.ds(q0, nb), c], ref[1, pl.ds(q0, nb), c]).reshape(TB, C)

    def put(ref, c, q0, value):
        value = value.reshape(nb, 2, 8, C)
        ref[0, pl.ds(q0, nb), c] = value[:, 0]
        ref[1, pl.ds(q0, nb), c] = value[:, 1]

    def places(c, j):
        q0 = pl.multiple_of(j * nb, nb)
        return q0, pl.ds(pl.multiple_of(c * H * 2 + j * TB, TB), TB)

    loads[LOC].wait()
    for c in range(2):
        def pre(j, carry):
            q0, rows = places(c, j)
            c16 = tokens(ocv, c, q0).astype(bf16)
            cot[rows, :] = c16
            dhid[rows, :] = mm_nt(c16, wdn[...].reshape(N, C))
            return carry

        lax.fori_loop(0, tiles, pre, 0)

    for c in range(2):
        from_core(A2 + c, 1, c)

        def mlp(j, carry):
            tile = lax.rem(lax.div(q, nb) + j, tiles)
            q0, rows = places(c, tile)
            mixed = ra[1, pl.ds(c * NQ + q0, nb)].reshape(TB, C).astype(f32)
            inp = tokens(xv, c, q0)
            gate = jax.nn.sigmoid(inp)
            branch = inp + gate * mixed
            put(out_ref, c, q0, branch)
            normed = branch.astype(bf16)
            nrm[rows, :] = normed
            up = mm(normed, wup[...])
            active, slope = gelu_parts(up)
            hid[rows, :] = active.astype(bf16)
            d_up = (dhid[rows, :] * slope).astype(bf16)
            dup[rows, :] = d_up
            d_branch = tokens(ocv, c, q0) + mm_nt(d_up, wup[...])
            sa[2, pl.ds(c * NQ + q0, nb)] = (d_branch * gate).astype(bf16).reshape(nb, 16, C)

            def one(b, inner):
                peer = q0 + lax.rem(q + b, nb)

                @pl.when((peer != q) | (core != c))
                def _():
                    push(A3, sa.at[2, c * NQ + peer], ra.at[2, me], 2 * peer + c, y)

                return inner

            lax.fori_loop(0, nb, one, 0)
            put(gx_ref, c, q0, d_branch * (1.0 + gate * (1.0 - gate) * mixed))
            return carry

        lax.fori_loop(0, tiles, mlp, 0)
    ra[2, me] = sa[2, me]

    from_all(A3, 2)
    grad = ra[2].reshape(N, C)
    sa[3] = (mm(kth[...], grad) + mm(ktl[...], grad)).astype(bf16).reshape(nt, 16, C)
    ra[3, me] = sa[3, me]
    a2a(3, A4 + core)

    gd_part = mm_tn(hid[...], cot[...]).reshape(NQ, 2, 16, C)
    for c in range(2):
        gbuf[c, :, 0:16] = gd_part[:, c]
    for fq in range(4):
        gu_part = mm_tn(nrm[...], dup[:, fq * C : (fq + 1) * C])
        for h in range(C // W):
            stage[...] = gu_part[:, h * W : (h + 1) * W]
            for r in range(4):
                rows4[h, pl.ds(4 * fq + r, nt, stride=16), :] = stage[pl.ds(r, nt, stride=4), :]
    for c in range(2):
        for h in range(C // W):
            gbuf[c, :, 16:32, h * W : (h + 1) * W] = rows4[h].reshape(NQ, 2, 16, W)[:, c]
    push(GC, gbuf.at[other], rgc, sib, y)

    tsum[...] = jnp.zeros((R, R), f32)

    def two(b, carry):
        r0 = pl.multiple_of(b * band, band)
        blocks = ra[2, pl.ds(b * (band // 16), band // 16)]
        prod = mm_nt(blocks.reshape(band, C), ra[0].reshape(N, C))
        ph, pw = split(jnp.where(same, prod, 0.0))
        ph, pw = split(mm(ph, spread) + mm(pw, spread))
        tsum[...] += mm_tn(picked(r0), ph) + mm_tn(picked(r0), pw)
        return carry

    lax.fori_loop(0, N // band, two, 0)
    tpart[...] = tsum[...].reshape(2, nt, R)
    push(TC, tpart.at[other], rtc, sib, y)

    arrive(GC, rgc)
    sgx[...] = (gbuf[core] + rgc[...]).astype(bf16).reshape(X, Z, 32, C)

    def send_gx(d):
        peer = lax.rem(xx + d, X)
        push(GX, sgx.at[peer], rgx.at[xx], tok_of(peer, z), y)

    each(X, send_gx)

    arrive(TC, rtc)
    stz[...] = (tpart[core] + rtc[...]).reshape(Z, nt // Z, R)

    def send_tz(d):
        peer = lax.rem(z + d, Z)
        push(TZ, stz.at[peer], rtz.at[z], tok_of(xx, peer), y)

    each(Z, send_tz)

    for c in range(2):
        def finish(j, carry):
            q0, rows = places(c, j)
            put(out_ref, c, q0, tokens(out_ref, c, q0) + mm(hid[rows, :], wdn[...].reshape(N, C)))
            return carry

        lax.fori_loop(0, tiles, finish, 0)

    arrive(GX, rgx.at[pl.ds(0, X - 1)])
    rgx[xx] = jnp.zeros((Z, 32, C), bf16)
    zrows = pl.ds(xx * Z, Z)
    own_gz = gbuf[core, zrows] + rgc[zrows]
    for s in range(X):
        own_gz = own_gz + rgx[s].astype(f32)
    gbuf[core, zrows] = own_gz
    sgz[...] = own_gz.astype(bf16)

    def send_gz(d):
        peer = lax.rem(z + d, Z)
        push(GZ, sgz.at[peer], rgz.at[z], tok_of(xx, peer), y)

    each(Z, send_gz)

    arrive(TZ, rtz.at[pl.ds(0, Z - 1)])
    rtz[z] = stz[z]
    rtx[xx] = rtz[...].sum(axis=0)
    each(X, lambda d: push(TX, rtx.at[xx], rtx.at[xx], tok_of(lax.rem(xx + d, X), z), y))

    for c in range(2):
        from_core(A4 + c, 3, c)
        d_mid = ra[3, c * NQ : (c + 1) * NQ].astype(f32).reshape(NQ, 2, 8, C)
        one = None
        for i in range(2):
            d_first = (d_mid[:, i] * twc[i, :, c]).reshape(H, C).astype(bf16)
            df[c, i] = d_first
            part = mm_nt(d_first, xb[i])
            one = part if one is None else one + part
        one = one.reshape(NQ, 8, M)
        for v in range(Y):
            ppart[c, v] = one[:, :, v * LY : (v + 1) * LY]

        @pl.when(core != c)
        def _():
            push(PC, ppart.at[c], rpc, sib, y)

    arrive(PC, rpc)
    spy[...] = (ppart[core] + rpc[...]).astype(bf16).reshape(Y, NQ * 8, LY)

    def send_py(d):
        peer = lax.rem(y + d, Y)
        push(PY, spy.at[peer], rpy.at[y], t, peer)

    each(Y, send_py)

    arrive(TX, rtx.at[pl.ds(0, X - 1)])
    rty[y] = rtx[...].sum(axis=0)
    each(Y, lambda d: push(TY, rty.at[y], rty.at[y], t, lax.rem(y + d, Y)))

    arrive(GZ, rgz.at[pl.ds(0, Z - 1)])
    rgz[z] = jnp.zeros((32, C), bf16)
    wpack[...] = gbuf[core, xx * Z + z] + rgz[...].astype(f32).sum(axis=0)
    gd_ref[...] = wpack[0:16, :]
    for fq in range(4):
        gu_ref[:, fq * C : (fq + 1) * C] = wpack[16 + 4 * fq : 20 + 4 * fq, :]

    arrive(PY, rpy.at[pl.ds(0, Y - 1)])
    rpy[y] = jnp.zeros((NQ * 8, LY), bf16)
    total = (ppart[core, y] + rpc[y]).reshape(NQ * 8, LY)
    for s in range(Y):
        total = total + rpy[s].astype(f32)
    spq[...] = total.reshape(NQ, 8, LY)

    def send_pq(d):
        peer = lax.rem(q + d, NQ)
        push(PQ, spq.at[peer], rpq.at[q], 2 * peer + core, y)

    each(NQ, send_pq)

    arrive(TY, rty.at[pl.ds(0, Y - 1)])
    rt2[core, z] = rty[...].sum(axis=0)
    each(Z, lambda d: push(TZ2, rt2.at[core, z], rt2.at[core, z], tok_of(xx, lax.rem(z + d, Z)), y))

    for i in range(2):
        d_grid = mm(f1t[0], df[0, i]) + mm(f1t[1], df[1, i])
        gx_ref[i] = gx_ref[i] + d_grid.reshape(NQ, 2, 8, C)

    arrive(PQ, rpq.at[pl.ds(0, NQ - 1)])
    rpq[q] = spq[q]
    fin[q] = rpq[...].sum(axis=0).astype(bf16).astype(f32)
    each(NQ, lambda d: push(PQ2, fin.at[q], fin.at[q], 2 * lax.rem(q + d, NQ) + core, y))

    arrive(TZ2, rt2.at[core, pl.ds(0, Z - 1)])
    push(TC2, rt2.at[core], rt2.at[core], sib, y)

    arrive(PQ2, fin.at[pl.ds(0, NQ - 1)])
    fy[core, y] = fin[...].reshape(NQ * 8, LY).astype(bf16)
    each(Y, lambda d: push(PY2, fy.at[core, y], fy.at[core, y], t, lax.rem(y + d, Y)))
    arrive(TC2, rt2.at[other])
    g2_ref[...] = rt2[...].reshape(R, R)
    arrive(PY2, fy.at[core, pl.ds(0, Y - 1)])
    push(PC2, fy.at[core], fy.at[core], sib, y)
    arrive(PC2, fy.at[other])

    for which, phase in ((A1, 0), (A2 + core, 1), (A3, 2), (A4 + core, 3)):
        sent(which, sa.at[phase, pl.ds(0, nt - 1)])
    sent(WZ, wbuf.at[0, 0, pl.ds(0, Z - 1)])
    sent(WX, wbuf.at[0, pl.ds(0, X - 1)])
    sent(WC, wbuf.at[0])
    sent(GC, rgc)
    sent(GX, sgx.at[pl.ds(0, X - 1)])
    sent(GZ, sgz.at[pl.ds(0, Z - 1)])
    sent(TC, rtc)
    sent(TZ, stz.at[pl.ds(0, Z - 1)])
    sent(TX, rtx.at[pl.ds(0, X - 1)])
    sent(TY, rty.at[pl.ds(0, Y - 1)])
    sent(TZ2, rt2.at[0, pl.ds(0, Z - 1)])
    sent(TC2, rt2.at[0])
    sent(PC, rpc)
    sent(PY, spy.at[pl.ds(0, Y - 1)])
    sent(PQ, spq.at[pl.ds(0, NQ - 1)])
    sent(PQ2, fin.at[pl.ds(0, NQ - 1)])
    sent(PY2, fy.at[0, pl.ds(0, Y - 1)])
    sent(PC2, fy.at[0])


def deliver(Y, out_in, gx_in, fy_in, g2_in, gu_in, gd_in,
            out_ref, gx_ref, g1_ref, g2_ref, gu_ref, gd_ref, whole, sem):
    copies = [pltpu.make_async_copy(src, dst, sem.at[n]) for n, (src, dst) in enumerate(
        ((out_in, out_ref), (gx_in, gx_ref), (g2_in, g2_ref), (gu_in, gu_ref), (gd_in, gd_ref)))]
    for copy in copies:
        copy.start()
    NQ = whole.shape[0]
    LY = whole.shape[3] // Y
    for c in range(2):
        for v in range(Y):
            whole[:, c, :, v * LY : (v + 1) * LY] = fy_in[c, v].astype(f32).reshape(NQ, 8, LY)
    last = pltpu.make_async_copy(whole, g1_ref, sem.at[5])
    last.start()
    for copy in copies:
        copy.wait()
    last.wait()


def local(X, Z, Y, inputs, factor_one, twiddle, factor_two, w_up, w_down, out_cotangent):
    NQ = X * Z
    nt = 2 * NQ
    C = inputs.shape[1]
    M = 8 * nt
    H = 8 * NQ
    N = 16 * nt
    R = 2 * nt
    LY = M // Y
    W = min(C, 128)
    V = pltpu.VMEM
    whole = (2, NQ, 2, 8, C)
    scratch = [
        V(whole, f32), V((M, M), f32), V(whole, f32), V((2, M), f32), V((R, R), f32),
        V((4, 4 * C), bf16), V((16, C), bf16),
        V((4, nt, 16, C), bf16), V((4, nt, 16, C), bf16),
        V((N, N), bf16), V((N, N), bf16), V((N, N), bf16),
        V((2, M, H), bf16), V((2, M, C), bf16), V((2, NQ, 2, 8, 1), f32),
        V((2, X, Z, 32, C), bf16), V((C, 4 * C), bf16), V((NQ, 2, 16, C), bf16),
        V((C, W), f32), V((C // W, N, W), f32),
        V((N, 4 * C), f32), V((N, 4 * C), bf16), V((N, 4 * C), bf16), V((N, C), bf16), V((N, C), bf16),
        V((2, 2, H, C), bf16),
        V((2, NQ, 32, C), f32), V((NQ, 32, C), f32),
        V((X, Z, 32, C), bf16), V((X, Z, 32, C), bf16), V((Z, 32, C), bf16), V((Z, 32, C), bf16),
        V((R, R), f32), V((2, nt, R), f32), V((nt, R), f32),
        V((Z, nt // Z, R), f32), V((Z, nt // Z, R), f32), V((X, nt // Z, R), f32), V((Y, nt // Z, R), f32),
        V((2, Z, nt // Z, R), f32),
        V((2, Y, NQ, 8, LY), f32), V((Y, NQ, 8, LY), f32),
        V((Y, NQ * 8, LY), bf16), V((Y, NQ * 8, LY), bf16),
        V((NQ, 8, LY), f32), V((NQ, 8, LY), f32), V((NQ, 8, LY), f32),
        V((32, C), f32),
        pltpu.SemaphoreType.DMA((NEX,)), pltpu.SemaphoreType.DMA((NEX,)), pltpu.SemaphoreType.DMA((7,)),
    ]
    small = [((R, R), f32), ((4, 4 * C), f32), ((16, C), f32)]
    held = [(whole, f32), (whole, f32), ((2, Y, NQ * 8, LY), bf16)] + small
    final = [(whole, f32), (whole, f32), ((NQ, 2, 8, M), f32)] + small
    vm = pl.BlockSpec(memory_space=pltpu.VMEM)
    anywhere = pl.BlockSpec(memory_space=pl.ANY)
    results = pl.pallas_call(
        functools.partial(kernel, X, Z, Y),
        out_shape=[pltpu.VMEM(*s) for s in held],
        in_specs=[anywhere] * 7,
        out_specs=[vm] * 6,
        scratch_shapes=scratch,
        compiler_params=pltpu.CompilerParams(
            collective_id=0, has_side_effects=True, vmem_limit_bytes=60 * 1024 * 1024),
        name="monarch",
    )(
        inputs.reshape(whole), factor_one, twiddle, factor_two,
        w_up[0], w_down[0], out_cotangent.reshape(whole),
    )
    out, gx, g1, g2, gu, gd = pl.pallas_call(
        functools.partial(deliver, Y),
        out_shape=[jax.ShapeDtypeStruct(*s) for s in final],
        in_specs=[vm] * 6,
        out_specs=[anywhere] * 6,
        scratch_shapes=[V((NQ, 2, 8, M), f32), pltpu.SemaphoreType.DMA((6,))],
        compiler_params=pltpu.CompilerParams(vmem_limit_bytes=8 * 1024 * 1024),
        name="deliver",
    )(*[pltpu.with_memory_space_constraint(r, pltpu.VMEM) for r in results])
    return (out.reshape(2 * M, C), gx.reshape(2 * M, C), g1.reshape(M, M), g2, gu[None], gd[None])


def solution(mesh):
    nt = mesh.shape["tok"]
    Y = mesh.shape["ch"]
    X = 4 if nt == 64 else 2
    in_specs = (
        P("tok", "ch"),
        P(),
        P("tok", None),
        P(),
        P("ch", "tok", None),
        P("ch", "tok", None),
        P("tok", "ch"),
    )
    out_specs = (
        P("tok", "ch"),
        P("tok", "ch"),
        P(),
        P(),
        P("ch", "tok", None),
        P("ch", "tok", None),
    )
    return jax.shard_map(
        functools.partial(local, X, nt // 2 // X, Y), mesh=mesh, in_specs=in_specs, out_specs=out_specs, check_vma=False)
```

time: 134 us -> 113 us (0.84)
  Pallas kernels: 126 us -> 113 us
  local copies, waits for them, and re-layouts: 6.98 us -> 0 us
    pallas_call x1 -> x2, Pallas kernels: 126 us -> 113 us  [the longest x1 111 us: local(): pl.pallas_call(functools.partial(kernel, X, Z, Y), out_shape=[pltpu.VMEM(...]
    unnamed x16 -> x0, local copies, waits for them, and re-layouts: 6.98 us -> none
where the time goes in v2:
time: 113 us
  Pallas kernels  113 us (100%)
    pallas_call x1, Pallas kernels, local(): pl.pallas_call(functools.partial(kernel, X, Z, Y), out_shape=[pltpu.VMEM(...  111 us

profile of v2, /device:TPU:1, one launch (start us, length us, event | category | flops | bytes accessed | tf_op | source)
XLA Modules:
  0.0 113.4 jit_solution(9279352954378741162)
XLA Ops:
  0.6 111.0 %monarch.1 = (f32[2,32,2,8,256]{4,3,2,1,0:T(8,128)S(1)}, f32[2,32,2,8,256]{4,3,2,1,0:T(8,128)S(1)}, bf16[2,4,256,128]{3,2,1,0:T(8,128)(2,1)S(1)}, f32[128,128]{1...) custom-call(f32[2,32,2,8,256]{4,3,2,1,0:T(8,128)} %bitcast.9, f32[512,512]{1,0:T(8,128)} %f1_in.1, ...), custom_call_target="tpu_custom_call" | custom-call | tf_op jit(solution)/shard_map/monarch/pallas_call | solution.py:515
  111.6 1.7 %deliver.1 = (f32[2,32,2,8,256]{4,3,2,1,0:T(8,128)}, f32[2,32,2,8,256]{4,3,2,1,0:T(8,128)}, f32[32,2,8,512]{3,2,1,0:T(8,128)}, f32[128,128]{1,0:T(8,128)}, f32[4,1024]{1,0:T(4,128)}, /*index=5*/f32[16,256]{1,0:T(8,128)}) custom-call(f32[2,32,2,8,256]{4,3,2,1,0:T(8,128)S(1)} %get-tuple-element.18.out_in, f32[2,32,2,8,256]{4,3,2,1,0:T(8,128)S(1)} %get-tuple-element.19.gx_in, ...), custom_call_target="tpu_custom_call" | custom-call | tf_op jit(solution)/shard_map/deliver/pallas_call | solution.py:528

commit v3 on v2

--- a/solution.py
+++ b/solution.py
@@ -132,34 +132,6 @@
         [wd_ref[...].astype(f32)] + [wu_ref[:, fq * C : (fq + 1) * C].astype(f32) for fq in range(4)], axis=0)
     wbuf[core, xx, z] = wpack[...].astype(bf16)
 
-    pl.semaphore_wait(barrier, nt - 1 + Y - 1)
-
-    def a2a(phase, which):
-        for c in range(2):
-            def one(d):
-                peer = lax.rem(q + d, NQ)
-
-                @pl.when((peer != q) | (core != c))
-                def _():
-                    push(which, sa.at[phase, c * NQ + peer], ra.at[phase, me], 2 * peer + c, y)
-
-            each(NQ, one, 0)
-
-    def from_core(which, phase, c):
-        @pl.when(core == c)
-        def _():
-            arrive(which, ra.at[phase, pl.ds(0, NQ - 1)])
-
-        @pl.when(core != c)
-        def _():
-            arrive(which, ra.at[phase, pl.ds(0, NQ)])
-
-    def from_all(which, phase):
-        arrive(which, ra.at[phase, pl.ds(0, nt - 1)])
-
-    a2a(0, A1)
-    each(Z, lambda d: push(WZ, wbuf.at[core, xx, z], wbuf.at[core, xx, z], tok_of(xx, lax.rem(z + d, Z)), y))
-
     loads[LF2].wait()
     f2h = f2v[...].astype(bf16)
     f2th, f2tl = split(f2v[...].T)
@@ -186,9 +158,39 @@
 
     build(f2h, kh)
 
+    pl.semaphore_wait(barrier, nt - 1 + Y - 1)
+
+    def a2a(phase, which):
+        for c in range(2):
+            def one(d):
+                peer = lax.rem(q + d, NQ)
+
+                @pl.when((peer != q) | (core != c))
+                def _():
+                    push(which, sa.at[phase, c * NQ + peer], ra.at[phase, me], 2 * peer + c, y)
+
+            each(NQ, one, 0)
+
+    def from_core(which, phase, c):
+        @pl.when(core == c)
+        def _():
+            arrive(which, ra.at[phase, pl.ds(0, NQ - 1)])
+
+        @pl.when(core != c)
+        def _():
+            arrive(which, ra.at[phase, pl.ds(0, NQ)])
+
+    def from_all(which, phase):
+        arrive(which, ra.at[phase, pl.ds(0, nt - 1)])
+
+    each(Z, lambda d: push(WZ, wbuf.at[core, xx, z], wbuf.at[core, xx, z], tok_of(xx, lax.rem(z + d, Z)), y))
+    a2a(0, A1)
+    build(f2th, kth)
+
     arrive(WZ, wbuf.at[core, xx, pl.ds(0, Z - 1)])
     each(X, lambda d: push(WX, wbuf.at[core, xx], wbuf.at[core, xx], tok_of(lax.rem(xx + d, X), z), y))
 
+    build(f2tl, ktl)
     from_all(A1, 0)
     sa[1] = mm(kh[...], ra[0].reshape(N, C)).astype(bf16).reshape(nt, 16, C)
     ra[1, me] = sa[1, me]
@@ -196,8 +198,6 @@
 
     arrive(WX, wbuf.at[core, pl.ds(0, X - 1)])
     push(WC, wbuf.at[core], wbuf.at[core], sib, y)
-    build(f2th, kth)
-    build(f2tl, ktl)
     for c in range(2):
         f1t[c] = f1v[...].reshape(NQ, 2, 8, M)[:, c].reshape(H, M).T.astype(bf16)
     arrive(WC, wbuf.at[other])
@@ -332,34 +332,6 @@
     each(Z, send_tz)
 
     for c in range(2):
-        def finish(j, carry):
-            q0, rows = places(c, j)
-            put(out_ref, c, q0, tokens(out_ref, c, q0) + mm(hid[rows, :], wdn[...].reshape(N, C)))
-            return carry
-
-        lax.fori_loop(0, tiles, finish, 0)
-
-    arrive(GX, rgx.at[pl.ds(0, X - 1)])
-    rgx[xx] = jnp.zeros((Z, 32, C), bf16)
-    zrows = pl.ds(xx * Z, Z)
-    own_gz = gbuf[core, zrows] + rgc[zrows]
-    for s in range(X):
-        own_gz = own_gz + rgx[s].astype(f32)
-    gbuf[core, zrows] = own_gz
-    sgz[...] = own_gz.astype(bf16)
-
-    def send_gz(d):
-        peer = lax.rem(z + d, Z)
-        push(GZ, sgz.at[peer], rgz.at[z], tok_of(xx, peer), y)
-
-    each(Z, send_gz)
-
-    arrive(TZ, rtz.at[pl.ds(0, Z - 1)])
-    rtz[z] = stz[z]
-    rtx[xx] = rtz[...].sum(axis=0)
-    each(X, lambda d: push(TX, rtx.at[xx], rtx.at[xx], tok_of(lax.rem(xx + d, X), z), y))
-
-    for c in range(2):
         from_core(A4 + c, 3, c)
         d_mid = ra[3, c * NQ : (c + 1) * NQ].astype(f32).reshape(NQ, 2, 8, C)
         one = None
@@ -376,6 +348,14 @@
         def _():
             push(PC, ppart.at[c], rpc, sib, y)
 
+    for c in range(2):
+        def finish(j, carry):
+            q0, rows = places(c, j)
+            put(out_ref, c, q0, tokens(out_ref, c, q0) + mm(hid[rows, :], wdn[...].reshape(N, C)))
+            return carry
+
+        lax.fori_loop(0, tiles, finish, 0)
+
     arrive(PC, rpc)
     spy[...] = (ppart[core] + rpc[...]).astype(bf16).reshape(Y, NQ * 8, LY)
 
@@ -384,6 +364,43 @@
         push(PY, spy.at[peer], rpy.at[y], t, peer)
 
     each(Y, send_py)
+
+    arrive(GX, rgx.at[pl.ds(0, X - 1)])
+    rgx[xx] = jnp.zeros((Z, 32, C), bf16)
+    zrows = pl.ds(xx * Z, Z)
+    own_gz = gbuf[core, zrows] + rgc[zrows]
+    for s in range(X):
+        own_gz = own_gz + rgx[s].astype(f32)
+    gbuf[core, zrows] = own_gz
+    sgz[...] = own_gz.astype(bf16)
+
+    def send_gz(d):
+        peer = lax.rem(z + d, Z)
+        push(GZ, sgz.at[peer], rgz.at[z], tok_of(xx, peer), y)
+
+    each(Z, send_gz)
+
+    arrive(TZ, rtz.at[pl.ds(0, Z - 1)])
+    rtz[z] = stz[z]
+    rtx[xx] = rtz[...].sum(axis=0)
+    each(X, lambda d: push(TX, rtx.at[xx], rtx.at[xx], tok_of(lax.rem(xx + d, X), z), y))
+
+    arrive(PY, rpy.at[pl.ds(0, Y - 1)])
+    rpy[y] = jnp.zeros((NQ * 8, LY), bf16)
+    total = (ppart[core, y] + rpc[y]).reshape(NQ * 8, LY)
+    for s in range(Y):
+        total = total + rpy[s].astype(f32)
+    spq[...] = total.reshape(NQ, 8, LY)
+
+    def send_pq(d):
+        peer = lax.rem(q + d, NQ)
+        push(PQ, spq.at[peer], rpq.at[q], 2 * peer + core, y)
+
+    each(NQ, send_pq)
+
+    for i in range(2):
+        d_grid = mm(f1t[0], df[0, i]) + mm(f1t[1], df[1, i])
+        gx_ref[i] = gx_ref[i] + d_grid.reshape(NQ, 2, 8, C)
 
     arrive(TX, rtx.at[pl.ds(0, X - 1)])
     rty[y] = rtx[...].sum(axis=0)
@@ -396,42 +413,24 @@
     for fq in range(4):
         gu_ref[:, fq * C : (fq + 1) * C] = wpack[16 + 4 * fq : 20 + 4 * fq, :]
 
-    arrive(PY, rpy.at[pl.ds(0, Y - 1)])
-    rpy[y] = jnp.zeros((NQ * 8, LY), bf16)
-    total = (ppart[core, y] + rpc[y]).reshape(NQ * 8, LY)
-    for s in range(Y):
-        total = total + rpy[s].astype(f32)
-    spq[...] = total.reshape(NQ, 8, LY)
-
-    def send_pq(d):
-        peer = lax.rem(q + d, NQ)
-        push(PQ, spq.at[peer], rpq.at[q], 2 * peer + core, y)
-
-    each(NQ, send_pq)
-
-    arrive(TY, rty.at[pl.ds(0, Y - 1)])
-    rt2[core, z] = rty[...].sum(axis=0)
-    each(Z, lambda d: push(TZ2, rt2.at[core, z], rt2.at[core, z], tok_of(xx, lax.rem(z + d, Z)), y))
-
-    for i in range(2):
-        d_grid = mm(f1t[0], df[0, i]) + mm(f1t[1], df[1, i])
-        gx_ref[i] = gx_ref[i] + d_grid.reshape(NQ, 2, 8, C)
-
     arrive(PQ, rpq.at[pl.ds(0, NQ - 1)])
     rpq[q] = spq[q]
     fin[q] = rpq[...].sum(axis=0).astype(bf16).astype(f32)
     each(NQ, lambda d: push(PQ2, fin.at[q], fin.at[q], 2 * lax.rem(q + d, NQ) + core, y))
 
-    arrive(TZ2, rt2.at[core, pl.ds(0, Z - 1)])
-    push(TC2, rt2.at[core], rt2.at[core], sib, y)
+    arrive(TY, rty.at[pl.ds(0, Y - 1)])
+    rt2[core, z] = rty[...].sum(axis=0)
+    each(Z, lambda d: push(TZ2, rt2.at[core, z], rt2.at[core, z], tok_of(xx, lax.rem(z + d, Z)), y))
 
     arrive(PQ2, fin.at[pl.ds(0, NQ - 1)])
     fy[core, y] = fin[...].reshape(NQ * 8, LY).astype(bf16)
     each(Y, lambda d: push(PY2, fy.at[core, y], fy.at[core, y], t, lax.rem(y + d, Y)))
+    arrive(TZ2, rt2.at[core, pl.ds(0, Z - 1)])
+    push(TC2, rt2.at[core], rt2.at[core], sib, y)
+    arrive(PY2, fy.at[core, pl.ds(0, Y - 1)])
+    push(PC2, fy.at[core], fy.at[core], sib, y)
     arrive(TC2, rt2.at[other])
     g2_ref[...] = rt2[...].reshape(R, R)
-    arrive(PY2, fy.at[core, pl.ds(0, Y - 1)])
-    push(PC2, fy.at[core], fy.at[core], sib, y)
     arrive(PC2, fy.at[other])
 
     for which, phase in ((A1, 0), (A2 + core, 1), (A3, 2), (A4 + core, 3)):

time: 113 us -> 100 us (0.88)
  Pallas kernels: 113 us -> 99.3 us
    pallas_call x1, Pallas kernels: 111 us -> 97.5 us  [local(): pl.pallas_call(functools.partial(kernel, X, Z, Y), out_shape=[pltpu.VMEM(...]
where the time goes in v3:
time: 100 us; the launch traced here: 99.9 us
  Pallas kernels  99.3 us (99%)
    pallas_call x1, Pallas kernels, local(): pl.pallas_call(functools.partial(kernel, X, Z, Y), out_shape=[pltpu.VMEM(...  97.5 us

profile of v3, /device:TPU:1, one launch (start us, length us, event | category | flops | bytes accessed | tf_op | source)
XLA Modules:
  0.0 99.9 jit_solution(11831046580830631347)
XLA Ops:
  0.6 97.5 %monarch.1 = (f32[2,32,2,8,256]{4,3,2,1,0:T(8,128)S(1)}, f32[2,32,2,8,256]{4,3,2,1,0:T(8,128)S(1)}, bf16[2,4,256,128]{3,2,1,0:T(8,128)(2,1)S(1)}, f32[128,128]{1...) custom-call(f32[2,32,2,8,256]{4,3,2,1,0:T(8,128)} %bitcast.9, f32[512,512]{1,0:T(8,128)} %f1_in.1, ...), custom_call_target="tpu_custom_call" | custom-call | tf_op jit(solution)/shard_map/monarch/pallas_call | solution.py:514
  98.2 1.7 %deliver.1 = (f32[2,32,2,8,256]{4,3,2,1,0:T(8,128)}, f32[2,32,2,8,256]{4,3,2,1,0:T(8,128)}, f32[32,2,8,512]{3,2,1,0:T(8,128)}, f32[128,128]{1,0:T(8,128)}, f32[4,1024]{1,0:T(4,128)}, /*index=5*/f32[16,256]{1,0:T(8,128)}) custom-call(f32[2,32,2,8,256]{4,3,2,1,0:T(8,128)S(1)} %get-tuple-element.18.out_in, f32[2,32,2,8,256]{4,3,2,1,0:T(8,128)S(1)} %get-tuple-element.19.gx_in, ...), custom_call_target="tpu_custom_call" | custom-call | tf_op jit(solution)/shard_map/deliver/pallas_call | solution.py:527

commit v4 on v2

--- a/solution.py
+++ b/solution.py
@@ -43,9 +43,9 @@
 def kernel(X, Z, Y, x_in, f1_in, tw_in, f2_in, wu_in, wd_in, oc_in,
            out_ref, gx_ref, fy, g2_ref, gu_ref, gd_ref,
            xv, f1v, ocv, tw_ref, f2v, wu_ref, wd_ref,
-           sa, ra, kh, kth, ktl, f1t, xb, twc, wbuf, wup, wdn, stage, rows4, dhid, hid, dup, nrm, cot, df,
+           sa, ra, kh, kth, ktl, f1t, xb, xs, twc, wbuf, wup, wdn, stage, rows4, dhid, hid, dup, nrm, cot, df,
            gbuf, rgc, sgx, rgx, sgz, rgz, tsum, tpart, rtc, stz, rtz, rtx, rty, rt2,
-           ppart, rpc, spy, rpy, spq, rpq, fin, wpack, ssem, rsem, lsem):
+           pown, spc, rpc, spy, rpy, spq, rpq, wpack, ssem, rsem, lsem):
     NQ = X * Z
     nt = 2 * NQ
     C = xv.shape[4]
@@ -120,6 +120,7 @@
     for i in range(2):
         xh, xl = split(xv[i].reshape(M, C))
         xb[i] = xh
+        xs[i] = xl
         first = mm(f1h, xh) + mm(f1h, xl) + mm(f1l, xh)
         mids.append(first.reshape(NQ, 2, 8, C) * twc[i])
     for c in range(2):
@@ -157,8 +158,8 @@
     def from_all(which, phase):
         arrive(which, ra.at[phase, pl.ds(0, nt - 1)])
 
+    each(Z, lambda d: push(WZ, wbuf.at[core, xx, z], wbuf.at[core, xx, z], tok_of(xx, lax.rem(z + d, Z)), y))
     a2a(0, A1)
-    each(Z, lambda d: push(WZ, wbuf.at[core, xx, z], wbuf.at[core, xx, z], tok_of(xx, lax.rem(z + d, Z)), y))
 
     loads[LF2].wait()
     f2h = f2v[...].astype(bf16)
@@ -185,6 +186,7 @@
         lax.fori_loop(0, N // band, step, 0)
 
     build(f2h, kh)
+    build(f2th, kth)
 
     arrive(WZ, wbuf.at[core, xx, pl.ds(0, Z - 1)])
     each(X, lambda d: push(WX, wbuf.at[core, xx], wbuf.at[core, xx], tok_of(lax.rem(xx + d, X), z), y))
@@ -196,7 +198,6 @@
 
     arrive(WX, wbuf.at[core, pl.ds(0, X - 1)])
     push(WC, wbuf.at[core], wbuf.at[core], sib, y)
-    build(f2th, kth)
     build(f2tl, ktl)
     for c in range(2):
         f1t[c] = f1v[...].reshape(NQ, 2, 8, M)[:, c].reshape(H, M).T.astype(bf16)
@@ -313,24 +314,6 @@
     tpart[...] = tsum[...].reshape(2, nt, R)
     push(TC, tpart.at[other], rtc, sib, y)
 
-    arrive(GC, rgc)
-    sgx[...] = (gbuf[core] + rgc[...]).astype(bf16).reshape(X, Z, 32, C)
-
-    def send_gx(d):
-        peer = lax.rem(xx + d, X)
-        push(GX, sgx.at[peer], rgx.at[xx], tok_of(peer, z), y)
-
-    each(X, send_gx)
-
-    arrive(TC, rtc)
-    stz[...] = (tpart[core] + rtc[...]).reshape(Z, nt // Z, R)
-
-    def send_tz(d):
-        peer = lax.rem(z + d, Z)
-        push(TZ, stz.at[peer], rtz.at[z], tok_of(xx, peer), y)
-
-    each(Z, send_tz)
-
     for c in range(2):
         def finish(j, carry):
             q0, rows = places(c, j)
@@ -338,6 +321,87 @@
             return carry
 
         lax.fori_loop(0, tiles, finish, 0)
+
+    def send_py(d):
+        peer = lax.rem(y + d, Y)
+        push(PY, spy.at[peer], rpy.at[y], t, peer)
+
+    def over_cores():
+        arrive(PC, rpc)
+        pown[...] = pown[...] + rpc[...].astype(f32)
+        spy[...] = pown[...].astype(bf16)
+        each(Y, send_py)
+
+    for c in range(2):
+        from_core(A4 + c, 3, c)
+        d_mid = ra[3, c * NQ : (c + 1) * NQ].astype(f32).reshape(NQ, 2, 8, C)
+        one = None
+        for i in range(2):
+            d_first = (d_mid[:, i] * twc[i, :, c]).reshape(H, C).astype(bf16)
+            df[c, i] = d_first
+            part = mm_nt(d_first, xb[i]) + mm_nt(d_first, xs[i])
+            one = part if one is None else one + part
+        one = one.reshape(NQ, 8, M)
+
+        @pl.when(core != c)
+        def _():
+            for v in range(Y):
+                spc[v] = one[:, :, v * LY : (v + 1) * LY].astype(bf16)
+            push(PC, spc, rpc, sib, y)
+
+        @pl.when(core == c)
+        def _():
+            for v in range(Y):
+                pown[v] = one[:, :, v * LY : (v + 1) * LY]
+
+        if c == 0:
+            @pl.when(core == 0)
+            def _():
+                over_cores()
+
+    arrive(GC, rgc)
+    sgx[...] = (gbuf[core] + rgc[...]).astype(bf16).reshape(X, Z, 32, C)
+
+    def send_gx(d):
+        peer = lax.rem(xx + d, X)
+        push(GX, sgx.at[peer], rgx.at[xx], tok_of(peer, z), y)
+
+    each(X, send_gx)
+
+    arrive(TC, rtc)
+    stz[...] = (tpart[core] + rtc[...]).reshape(Z, nt // Z, R)
+
+    def send_tz(d):
+        peer = lax.rem(z + d, Z)
+        push(TZ, stz.at[peer], rtz.at[z], tok_of(xx, peer), y)
+
+    each(Z, send_tz)
+
+    @pl.when(core == 1)
+    def _():
+        over_cores()
+
+    arrive(TZ, rtz.at[pl.ds(0, Z - 1)])
+    rtz[z] = stz[z]
+    rtx[xx] = rtz[...].sum(axis=0)
+    each(X, lambda d: push(TX, rtx.at[xx], rtx.at[xx], tok_of(lax.rem(xx + d, X), z), y))
+
+    arrive(PY, rpy.at[pl.ds(0, Y - 1)])
+    rpy[y] = jnp.zeros((NQ, 8, LY), bf16)
+    total = pown[y]
+    for s in range(Y):
+        total = total + rpy[s].astype(f32)
+    spq[...] = total.astype(bf16)
+
+    def send_pq(d):
+        peer = lax.rem(q + d, NQ)
+        push(PQ, spq.at[peer], rpq.at[q], 2 * peer + core, y)
+
+    each(NQ, send_pq)
+
+    for i in range(2):
+        d_grid = mm(f1t[0], df[0, i]) + mm(f1t[1], df[1, i])
+        gx_ref[i] = gx_ref[i] + d_grid.reshape(NQ, 2, 8, C)
 
     arrive(GX, rgx.at[pl.ds(0, X - 1)])
     rgx[xx] = jnp.zeros((Z, 32, C), bf16)
@@ -354,40 +418,18 @@
 
     each(Z, send_gz)
 
-    arrive(TZ, rtz.at[pl.ds(0, Z - 1)])
-    rtz[z] = stz[z]
-    rtx[xx] = rtz[...].sum(axis=0)
-    each(X, lambda d: push(TX, rtx.at[xx], rtx.at[xx], tok_of(lax.rem(xx + d, X), z), y))
-
-    for c in range(2):
-        from_core(A4 + c, 3, c)
-        d_mid = ra[3, c * NQ : (c + 1) * NQ].astype(f32).reshape(NQ, 2, 8, C)
-        one = None
-        for i in range(2):
-            d_first = (d_mid[:, i] * twc[i, :, c]).reshape(H, C).astype(bf16)
-            df[c, i] = d_first
-            part = mm_nt(d_first, xb[i])
-            one = part if one is None else one + part
-        one = one.reshape(NQ, 8, M)
-        for v in range(Y):
-            ppart[c, v] = one[:, :, v * LY : (v + 1) * LY]
-
-        @pl.when(core != c)
-        def _():
-            push(PC, ppart.at[c], rpc, sib, y)
-
-    arrive(PC, rpc)
-    spy[...] = (ppart[core] + rpc[...]).astype(bf16).reshape(Y, NQ * 8, LY)
-
-    def send_py(d):
-        peer = lax.rem(y + d, Y)
-        push(PY, spy.at[peer], rpy.at[y], t, peer)
-
-    each(Y, send_py)
-
     arrive(TX, rtx.at[pl.ds(0, X - 1)])
     rty[y] = rtx[...].sum(axis=0)
     each(Y, lambda d: push(TY, rty.at[y], rty.at[y], t, lax.rem(y + d, Y)))
+
+    arrive(PQ, rpq.at[pl.ds(0, NQ - 1)])
+    rpq[q] = spq[q]
+    fy[core, y, q] = rpq[...].astype(f32).sum(axis=0).astype(bf16)
+    each(NQ, lambda d: push(PQ2, fy.at[core, y, q], fy.at[core, y, q], 2 * lax.rem(q + d, NQ) + core, y))
+
+    arrive(TY, rty.at[pl.ds(0, Y - 1)])
+    rt2[core, z] = rty[...].sum(axis=0)
+    each(Z, lambda d: push(TZ2, rt2.at[core, z], rt2.at[core, z], tok_of(xx, lax.rem(z + d, Z)), y))
 
     arrive(GZ, rgz.at[pl.ds(0, Z - 1)])
     rgz[z] = jnp.zeros((32, C), bf16)
@@ -396,42 +438,14 @@
     for fq in range(4):
         gu_ref[:, fq * C : (fq + 1) * C] = wpack[16 + 4 * fq : 20 + 4 * fq, :]
 
-    arrive(PY, rpy.at[pl.ds(0, Y - 1)])
-    rpy[y] = jnp.zeros((NQ * 8, LY), bf16)
-    total = (ppart[core, y] + rpc[y]).reshape(NQ * 8, LY)
-    for s in range(Y):
-        total = total + rpy[s].astype(f32)
-    spq[...] = total.reshape(NQ, 8, LY)
-
-    def send_pq(d):
-        peer = lax.rem(q + d, NQ)
-        push(PQ, spq.at[peer], rpq.at[q], 2 * peer + core, y)
-
-    each(NQ, send_pq)
-
-    arrive(TY, rty.at[pl.ds(0, Y - 1)])
-    rt2[core, z] = rty[...].sum(axis=0)
-    each(Z, lambda d: push(TZ2, rt2.at[core, z], rt2.at[core, z], tok_of(xx, lax.rem(z + d, Z)), y))
-
-    for i in range(2):
-        d_grid = mm(f1t[0], df[0, i]) + mm(f1t[1], df[1, i])
-        gx_ref[i] = gx_ref[i] + d_grid.reshape(NQ, 2, 8, C)
-
-    arrive(PQ, rpq.at[pl.ds(0, NQ - 1)])
-    rpq[q] = spq[q]
-    fin[q] = rpq[...].sum(axis=0).astype(bf16).astype(f32)
-    each(NQ, lambda d: push(PQ2, fin.at[q], fin.at[q], 2 * lax.rem(q + d, NQ) + core, y))
-
+    arrive(PQ2, fy.at[core, y, pl.ds(0, NQ - 1)])
+    each(Y, lambda d: push(PY2, fy.at[core, y], fy.at[core, y], t, lax.rem(y + d, Y)))
     arrive(TZ2, rt2.at[core, pl.ds(0, Z - 1)])
     push(TC2, rt2.at[core], rt2.at[core], sib, y)
-
-    arrive(PQ2, fin.at[pl.ds(0, NQ - 1)])
-    fy[core, y] = fin[...].reshape(NQ * 8, LY).astype(bf16)
-    each(Y, lambda d: push(PY2, fy.at[core, y], fy.at[core, y], t, lax.rem(y + d, Y)))
+    arrive(PY2, fy.at[core, pl.ds(0, Y - 1)])
+    push(PC2, fy.at[core], fy.at[core], sib, y)
     arrive(TC2, rt2.at[other])
     g2_ref[...] = rt2[...].reshape(R, R)
-    arrive(PY2, fy.at[core, pl.ds(0, Y - 1)])
-    push(PC2, fy.at[core], fy.at[core], sib, y)
     arrive(PC2, fy.at[other])
 
     for which, phase in ((A1, 0), (A2 + core, 1), (A3, 2), (A4 + core, 3)):
@@ -451,7 +465,7 @@
     sent(PC, rpc)
     sent(PY, spy.at[pl.ds(0, Y - 1)])
     sent(PQ, spq.at[pl.ds(0, NQ - 1)])
-    sent(PQ2, fin.at[pl.ds(0, NQ - 1)])
+    sent(PQ2, fy.at[0, 0, pl.ds(0, NQ - 1)])
     sent(PY2, fy.at[0, pl.ds(0, Y - 1)])
     sent(PC2, fy.at[0])
 
@@ -466,7 +480,7 @@
     LY = whole.shape[3] // Y
     for c in range(2):
         for v in range(Y):
-            whole[:, c, :, v * LY : (v + 1) * LY] = fy_in[c, v].astype(f32).reshape(NQ, 8, LY)
+            whole[:, c, :, v * LY : (v + 1) * LY] = fy_in[c, v].astype(f32)
     last = pltpu.make_async_copy(whole, g1_ref, sem.at[5])
     last.start()
     for copy in copies:
@@ -491,7 +505,7 @@
         V((4, 4 * C), bf16), V((16, C), bf16),
         V((4, nt, 16, C), bf16), V((4, nt, 16, C), bf16),
         V((N, N), bf16), V((N, N), bf16), V((N, N), bf16),
-        V((2, M, H), bf16), V((2, M, C), bf16), V((2, NQ, 2, 8, 1), f32),
+        V((2, M, H), bf16), V((2, M, C), bf16), V((2, M, C), bf16), V((2, NQ, 2, 8, 1), f32),
         V((2, X, Z, 32, C), bf16), V((C, 4 * C), bf16), V((NQ, 2, 16, C), bf16),
         V((C, W), f32), V((C // W, N, W), f32),
         V((N, 4 * C), f32), V((N, 4 * C), bf16), V((N, 4 * C), bf16), V((N, C), bf16), V((N, C), bf16),
@@ -501,14 +515,14 @@
         V((R, R), f32), V((2, nt, R), f32), V((nt, R), f32),
         V((Z, nt // Z, R), f32), V((Z, nt // Z, R), f32), V((X, nt // Z, R), f32), V((Y, nt // Z, R), f32),
         V((2, Z, nt // Z, R), f32),
-        V((2, Y, NQ, 8, LY), f32), V((Y, NQ, 8, LY), f32),
-        V((Y, NQ * 8, LY), bf16), V((Y, NQ * 8, LY), bf16),
-        V((NQ, 8, LY), f32), V((NQ, 8, LY), f32), V((NQ, 8, LY), f32),
+        V((Y, NQ, 8, LY), f32), V((Y, NQ, 8, LY), bf16), V((Y, NQ, 8, LY), bf16),
+        V((Y, NQ, 8, LY), bf16), V((Y, NQ, 8, LY), bf16),
+        V((NQ, 8, LY), bf16), V((NQ, 8, LY), bf16),
         V((32, C), f32),
         pltpu.SemaphoreType.DMA((NEX,)), pltpu.SemaphoreType.DMA((NEX,)), pltpu.SemaphoreType.DMA((7,)),
     ]
     small = [((R, R), f32), ((4, 4 * C), f32), ((16, C), f32)]
-    held = [(whole, f32), (whole, f32), ((2, Y, NQ * 8, LY), bf16)] + small
+    held = [(whole, f32), (whole, f32), ((2, Y, NQ, 8, LY), bf16)] + small
     final = [(whole, f32), (whole, f32), ((NQ, 2, 8, M), f32)] + small
     vm = pl.BlockSpec(memory_space=pltpu.VMEM)
     anywhere = pl.BlockSpec(memory_space=pl.ANY)

time: 113 us -> 96.6 us (0.85)
  Pallas kernels: 113 us -> 95.8 us
    pallas_call x1, Pallas kernels: 111 us -> 94.1 us  [local(): pl.pallas_call(functools.partial(kernel, X, Z, Y), out_shape=[pltpu.VMEM(...]
where the time goes in v4:
time: 96.6 us; the launch traced here: 96.5 us
  Pallas kernels  95.8 us (99%)
    pallas_call x1, Pallas kernels, local(): pl.pallas_call(functools.partial(kernel, X, Z, Y), out_shape=[pltpu.VMEM(...  94.1 us

profile of v4, /device:TPU:1, one launch (start us, length us, event | category | flops | bytes accessed | tf_op | source)
XLA Modules:
  0.0 96.5 jit_solution(13502805967585869099)
XLA Ops:
  0.6 94.1 %monarch.1 = (f32[2,32,2,8,256]{4,3,2,1,0:T(8,128)S(1)}, f32[2,32,2,8,256]{4,3,2,1,0:T(8,128)S(1)}, bf16[2,4,32,8,128]{4,3,2,1,0:T(8,128)(2,1)S(1)}, f32[128,128...) custom-call(f32[2,32,2,8,256]{4,3,2,1,0:T(8,128)} %bitcast.9, f32[512,512]{1,0:T(8,128)} %f1_in.1, ...), custom_call_target="tpu_custom_call" | custom-call | tf_op jit(solution)/shard_map/monarch/pallas_call | solution.py:529
  94.7 1.7 %deliver.1 = (f32[2,32,2,8,256]{4,3,2,1,0:T(8,128)}, f32[2,32,2,8,256]{4,3,2,1,0:T(8,128)}, f32[32,2,8,512]{3,2,1,0:T(8,128)}, f32[128,128]{1,0:T(8,128)}, f32[4,1024]{1,0:T(4,128)}, /*index=5*/f32[16,256]{1,0:T(8,128)}) custom-call(f32[2,32,2,8,256]{4,3,2,1,0:T(8,128)S(1)} %get-tuple-element.18.out_in, f32[2,32,2,8,256]{4,3,2,1,0:T(8,128)S(1)} %get-tuple-element.19.gx_in, ...), custom_call_target="tpu_custom_call" | custom-call | tf_op jit(solution)/shard_map/deliver/pallas_call | solution.py:542

commit v5 on v4

--- a/solution.py
+++ b/solution.py
@@ -44,7 +44,7 @@
            out_ref, gx_ref, fy, g2_ref, gu_ref, gd_ref,
            xv, f1v, ocv, tw_ref, f2v, wu_ref, wd_ref,
            sa, ra, kh, kth, ktl, f1t, xb, xs, twc, wbuf, wup, wdn, stage, rows4, dhid, hid, dup, nrm, cot, df,
-           gbuf, rgc, sgx, rgx, sgz, rgz, tsum, tpart, rtc, stz, rtz, rtx, rty, rt2,
+           gbuf, sgc, rgc, sgx, rgx, sgz, rgz, mid32, tpart, rtc, stz, rtz, rtx, rty, rt2,
            pown, spc, rpc, spy, rpy, spq, rpq, wpack, ssem, rsem, lsem):
     NQ = X * Z
     nt = 2 * NQ
@@ -189,16 +189,24 @@
     build(f2th, kth)
 
     arrive(WZ, wbuf.at[core, xx, pl.ds(0, Z - 1)])
-    each(X, lambda d: push(WX, wbuf.at[core, xx], wbuf.at[core, xx], tok_of(lax.rem(xx + d, X), z), y))
+    def send_wx(e):
+        d, part = 1 + lax.rem(e, X - 1), lax.div(e, X - 1)
+        push(WX, wbuf.at[core, xx, part], wbuf.at[core, xx, part], tok_of(lax.rem(xx + d, X), z), y)
+
+    each((X - 1) * Z, send_wx, 0)
 
     from_all(A1, 0)
-    sa[1] = mm(kh[...], ra[0].reshape(N, C)).astype(bf16).reshape(nt, 16, C)
+    mid = ra[0].reshape(N, C)
+    sa[1] = mm(kh[...], mid).astype(bf16).reshape(nt, 16, C)
     ra[1, me] = sa[1, me]
     a2a(1, A2 + core)
 
     arrive(WX, wbuf.at[core, pl.ds(0, X - 1)])
     push(WC, wbuf.at[core], wbuf.at[core], sib, y)
     build(f2tl, ktl)
+    mid = ra[0].reshape(N, C).astype(f32)
+    for h in range(C // W):
+        mid32[h] = mid[:, h * W : (h + 1) * W]
     for c in range(2):
         f1t[c] = f1v[...].reshape(NQ, 2, 8, M)[:, c].reshape(H, M).T.astype(bf16)
     arrive(WC, wbuf.at[other])
@@ -297,21 +305,22 @@
     for c in range(2):
         for h in range(C // W):
             gbuf[c, :, 16:32, h * W : (h + 1) * W] = rows4[h].reshape(NQ, 2, 16, W)[:, c]
-    push(GC, gbuf.at[other], rgc, sib, y)
-
-    tsum[...] = jnp.zeros((R, R), f32)
-
-    def two(b, carry):
-        r0 = pl.multiple_of(b * band, band)
-        blocks = ra[2, pl.ds(b * (band // 16), band // 16)]
-        prod = mm_nt(blocks.reshape(band, C), ra[0].reshape(N, C))
-        ph, pw = split(jnp.where(same, prod, 0.0))
-        ph, pw = split(mm(ph, spread) + mm(pw, spread))
-        tsum[...] += mm_tn(picked(r0), ph) + mm_tn(picked(r0), pw)
-        return carry
-
-    lax.fori_loop(0, N // band, two, 0)
-    tpart[...] = tsum[...].reshape(2, nt, R)
+    sgc[...] = gbuf[other].astype(bf16)
+    push(GC, sgc, rgc, sib, y)
+
+    grad = ra[2].reshape(N, C).astype(f32)
+    for h in range(C // W):
+        rows4[h] = grad[:, h * W : (h + 1) * W]
+    total = jnp.zeros((R, R), f32)
+    for k in range(8):
+        for h in range(C // W):
+            total = total + mm_nt(rows4[h, pl.ds(k, R, stride=8), :].astype(bf16),
+                                  mid32[h, pl.ds(k, R, stride=8), :].astype(bf16))
+    order = row_of(lax.broadcasted_iota(jnp.int32, (R, R), 0) * 8) == lax.broadcasted_iota(jnp.int32, (R, R), 1)
+    order = jnp.where(order, 1.0, 0.0).astype(bf16)
+    th, tl = split(total)
+    th, tl = split(mm(th, order) + mm(tl, order))
+    tpart[...] = (mm_tn(order, th) + mm_tn(order, tl)).reshape(2, nt, R)
     push(TC, tpart.at[other], rtc, sib, y)
 
     for c in range(2):
@@ -360,7 +369,7 @@
                 over_cores()
 
     arrive(GC, rgc)
-    sgx[...] = (gbuf[core] + rgc[...]).astype(bf16).reshape(X, Z, 32, C)
+    sgx[...] = (gbuf[core] + rgc[...].astype(f32)).astype(bf16).reshape(X, Z, 32, C)
 
     def send_gx(d):
         peer = lax.rem(xx + d, X)
@@ -406,7 +415,7 @@
     arrive(GX, rgx.at[pl.ds(0, X - 1)])
     rgx[xx] = jnp.zeros((Z, 32, C), bf16)
     zrows = pl.ds(xx * Z, Z)
-    own_gz = gbuf[core, zrows] + rgc[zrows]
+    own_gz = gbuf[core, zrows] + rgc[zrows].astype(f32)
     for s in range(X):
         own_gz = own_gz + rgx[s].astype(f32)
     gbuf[core, zrows] = own_gz
@@ -510,9 +519,9 @@
         V((C, W), f32), V((C // W, N, W), f32),
         V((N, 4 * C), f32), V((N, 4 * C), bf16), V((N, 4 * C), bf16), V((N, C), bf16), V((N, C), bf16),
         V((2, 2, H, C), bf16),
-        V((2, NQ, 32, C), f32), V((NQ, 32, C), f32),
+        V((2, NQ, 32, C), f32), V((NQ, 32, C), bf16), V((NQ, 32, C), bf16),
         V((X, Z, 32, C), bf16), V((X, Z, 32, C), bf16), V((Z, 32, C), bf16), V((Z, 32, C), bf16),
-        V((R, R), f32), V((2, nt, R), f32), V((nt, R), f32),
+        V((C // W, N, W), f32), V((2, nt, R), f32), V((nt, R), f32),
         V((Z, nt // Z, R), f32), V((Z, nt // Z, R), f32), V((X, nt // Z, R), f32), V((Y, nt // Z, R), f32),
         V((2, Z, nt // Z, R), f32),
         V((Y, NQ, 8, LY), f32), V((Y, NQ, 8, LY), bf16), V((Y, NQ, 8, LY), bf16),

time: 96.6 us -> 96.2 us (level)
  no operation moved by 1% of the time
where the time goes in v5:
time: 96.2 us; the launch traced here: 96.1 us
  Pallas kernels  95.5 us (99%)
    pallas_call x1, Pallas kernels, local(): pl.pallas_call(functools.partial(kernel, X, Z, Y), out_shape=[pltpu.VMEM(...  93.7 us

profile of v5, /device:TPU:1, one launch (start us, length us, event | category | flops | bytes accessed | tf_op | source)
XLA Modules:
  0.0 96.1 jit_solution(3472548352864149156)
XLA Ops:
  0.6 93.7 %monarch.1 = (f32[2,32,2,8,256]{4,3,2,1,0:T(8,128)S(1)}, f32[2,32,2,8,256]{4,3,2,1,0:T(8,128)S(1)}, bf16[2,4,32,8,128]{4,3,2,1,0:T(8,128)(2,1)S(1)}, f32[128,128...) custom-call(f32[2,32,2,8,256]{4,3,2,1,0:T(8,128)} %bitcast.9, f32[512,512]{1,0:T(8,128)} %f1_in.1, ...), custom_call_target="tpu_custom_call" | custom-call | tf_op jit(solution)/shard_map/monarch/pallas_call | solution.py:538
  94.4 1.7 %deliver.1 = (f32[2,32,2,8,256]{4,3,2,1,0:T(8,128)}, f32[2,32,2,8,256]{4,3,2,1,0:T(8,128)}, f32[32,2,8,512]{3,2,1,0:T(8,128)}, f32[128,128]{1,0:T(8,128)}, f32[4,1024]{1,0:T(4,128)}, /*index=5*/f32[16,256]{1,0:T(8,128)}) custom-call(f32[2,32,2,8,256]{4,3,2,1,0:T(8,128)S(1)} %get-tuple-element.18.out_in, f32[2,32,2,8,256]{4,3,2,1,0:T(8,128)S(1)} %get-tuple-element.19.gx_in, ...), custom_call_target="tpu_custom_call" | custom-call | tf_op jit(solution)/shard_map/deliver/pallas_call | solution.py:551
